TPU v7x, 256 devices: a whole 4x4x8 slice. The times are simulated.
256 devices in a mesh: island: 16 (over x, y), row: 4 (over z_hi), col: 4 (over z_lo, core).
Axes of the slice: x: 4, y: 4, z: 8 (z_hi: 4, z_lo: 2; z = z_hi * 2 + z_lo), core: 2. Of those that a mesh axis runs over, the one named last changes fastest.
Arguments:
- weights: float32 [16, 4096, 4096], P('island', 'row', 'col'), may hold values from -6 to 6
- bases: float32 [2, 32, 4096], P(None, None, 'col'), may hold values from -0.09375 to 0.09375
- pairs: int32 [2, 8, 2], replicated, may hold values from 0 to 15, as said below
Outputs:
- updated: float32 [16, 4096, 4096], P('island', 'row', 'col')
Inputs may be any that keep to these rules, and one draw needn't show every extreme that they name: In each matching every island appears exactly once among the pairs, so each matching is a perfect matching of the 16 islands.
All inputs are finite; a program needn't handle non-finite values.
Results may differ from a plain program's by a relative error of at most 0.00011.
Values sent between devices are 32-bit elements; how exact they have to be, the bound alone decides.
A program may use at most 64 MiB of HBM per device.

v0:
```python
import jax
import jax.numpy as jnp
from jax import lax
from jax.sharding import PartitionSpec as P

MATCHINGS = 2


def copy_for_each(array, axis):
    copies = jnp.broadcast_to(array, (lax.axis_size(axis), *array.shape))
    return lax.all_to_all(copies, axis, split_axis=0, concat_axis=0, tiled=True)


def in_order(blocks, dim):
    shape = list(blocks.shape[1:])
    shape[dim] *= blocks.shape[0]
    return jnp.moveaxis(blocks, 0, dim).reshape(shape)


def gathered_copies(array, axis, dim):
    blocks = copy_for_each(array, axis)
    return in_order(blocks, dim)


def split_up(array, dim, peers):
    shape = array.shape
    blocks = array.reshape(*shape[:dim], peers, shape[dim] // peers, *shape[dim + 1 :])
    return jnp.moveaxis(blocks, dim, 0)


def sum_at_owner(array, axis, dim):
    blocks = split_up(array, dim, lax.axis_size(axis))
    arrived = lax.all_to_all(blocks, axis, split_axis=0, concat_axis=0, tiled=True)
    return arrived.sum(axis=0)


def over_copies(array, axis):
    return copy_for_each(array, axis).sum(axis=0)


def partner_list(pair_rows, islands):
    positions = jnp.arange(islands, dtype=jnp.int32)
    first = pair_rows[:, 0]
    second = pair_rows[:, 1]
    from_first = jnp.where(first[None, :] == positions[:, None], second[None, :], 0)
    from_second = jnp.where(second[None, :] == positions[:, None], first[None, :], 0)
    return jnp.sum(from_first + from_second, axis=1)


def orthonormal(gram_matrix, left_factor):
    lower_factor = jnp.linalg.cholesky(gram_matrix)
    return jax.scipy.linalg.solve_triangular(lower_factor, left_factor, lower=True)


def combine_partner(values, partner_row, myself, factor_sign):
    islands = lax.axis_size("island")
    gathered = gathered_copies(values[None], "island", 0)
    positions = jnp.arange(islands, dtype=jnp.int32)
    mine = jnp.sum(jnp.where(positions == myself, partner_row, 0))
    partner_term = lax.dynamic_index_in_dim(gathered, mine, 0, keepdims=False)
    return values + factor_sign * partner_term


def shards(weights, bases, pairs):
    myself = lax.axis_index("island")
    islands = lax.axis_size("island")
    weight_tile = weights[0]
    for matching in range(MATCHINGS):
        base_rows = bases[matching]
        partner_row = partner_list(pairs[matching], islands)
        partial_terms = lax.dot_general(
            base_rows,
            weight_tile,
            (((1,), (1,)), ((), ())),
            precision=lax.Precision.HIGHEST,
            preferred_element_type=jnp.float32,
        )
        left_share = sum_at_owner(partial_terms, "col", 1)
        share_factor = combine_partner(left_share, partner_row, myself, -1.0)
        local_gram = jnp.dot(share_factor, share_factor.T, precision=lax.Precision.HIGHEST)
        gram_matrix = over_copies(local_gram, ("row", "col"))
        share_basis = orthonormal(gram_matrix, share_factor)
        left_basis = gathered_copies(share_basis, "col", 1)
        right_partial = jnp.dot(left_basis, weight_tile, precision=lax.Precision.HIGHEST)
        right_terms = over_copies(right_partial, "row")
        right_factor = combine_partner(right_terms, partner_row, myself, 1.0)
        correction = lax.dot_general(
            left_basis,
            right_factor,
            (((0,), (0,)), ((), ())),
            precision=lax.Precision.HIGHEST,
            preferred_element_type=jnp.float32,
        )
        weight_tile = weight_tile - 0.5 * correction
    return weight_tile[None]


def solution(mesh):
    in_specs = (P("island", "row", "col"), P(None, None, "col"), P())
    out_specs = P("island", "row", "col")
    return jax.shard_map(shards, mesh=mesh, in_specs=in_specs, out_specs=out_specs, check_vma=False)
```

profile of v0, /device:TPU:1, one launch (start us, length us, event | category | flops | bytes accessed | tf_op | source)
XLA Modules:
  0.0 234.8 jit_solution(6137875888489390332)
XLA Ops:
  0.0 6.1 %convolution_bitcast_fusion = f32[4,32,256]{2,1,0:T(8,128)S(1)} fusion(f32[4,256,1024]{2,1,0:T(8,128)} %bitcast.105, f32[2,32,1024]{2,1,0:T(8,128)} %param.7), kind=kOutput, calls=%fused_computation.4 | convolution fusion | flops 402653184 | bytes 4456448 | tf_op jit(solution)/shard_map/dot_general | solution.py:71
  6.1 9.2 %all_to_all.60 = f32[4,32,256]{2,1,0:T(8,128)S(1)} all-to-all(f32[4,32,256]{2,1,0:T(8,128)S(1)} %convolution_bitcast_fusion), channel_id=1, replica_groups=mesh['island'=16,'row'=4,'col'=4] {'col'}, dimensions={0} | all-to-all | bytes 262144 | tf_op jit(solution)/shard_map/all_to_all | solution.py:33
  16.2 5.6 %all-to-all-start.1 = ((f32[16,1,32,256]{3,2,1,0:T(8,128)}), f32[16,1,32,256]{3,2,1,0:T(8,128)S(1)}, u32[]{:S(2)}, u32[]{:S(2)}) async-start(f32[16,1,32,256]{3,2,1,0:T(8,128)} %broadcast_in_dim.79), calls=%async_computation.1 | async-start | bytes 1048576 | tf_op jit(solution)/shard_map/all_to_all | solution.py:11
  24.7 6.1 %all-to-all-done.1 = f32[16,1,32,256]{3,2,1,0:T(8,128)S(1)} async-done(((f32[16,1,32,256]{3,2,1,0:T(8,128)}), f32[16,1,32,256]{3,2,1,0:T(8,128)S(1)}, u32[]{:S(2)}, u32[]{:S(2)}) %all-to-all-start.1) | async-done | bytes 524320 | tf_op jit(solution)/shard_map/all_to_all | solution.py:11
  31.2 18.9 %all_to_all.61 = f32[16,1,1024]{2,1,0:T(1,128)S(1)} all-to-all(f32[16,1,1024]{2,1,0:T(1,128)S(1)} %reshape.56), channel_id=1, replica_groups=mesh['island'=16,'row'=4,'col'=4] {'row','col'}, dimensions={0} | all-to-all | bytes 131072 | tf_op jit(solution)/shard_map/all_to_all | solution.py:11
  51.8 2.9 %cholesky.44 = f32[32,32]{1,0:T(8,128)S(1)} custom-call(f32[32,32]{1,0:T(8,128)S(1)} %fusion.22), custom_call_target="Cholesky" | custom-call | tf_op jit(solution)/shard_map/jit(cholesky)/cholesky | solution.py:51
  56.0 2.4 %custom-call.6 = f32[1,32,32]{1,2,0:T(8,128)S(1)} custom-call(f32[1,32,32]{2,1,0:T(8,128)S(1)} %fusion.17), custom_call_target="InvertDiagBlocksLowerTriangular" | custom-call | tf_op jit(solution)/shard_map/jit(_solve_triangular)/triangular_solve | solution.py:52
  58.8 6.1 %all_to_all.62 = f32[4,32,256]{2,1,0:T(8,128)S(1)} all-to-all(f32[4,32,256]{2,1,0:T(8,128)S(1)} %broadcast_in_dim.85), channel_id=1, replica_groups=mesh['island'=16,'row'=4,'col'=4] {'col'}, dimensions={0} | all-to-all | bytes 262144 | tf_op jit(solution)/shard_map/all_to_all | solution.py:11
  64.9 4.7 %fusion = f32[32,1024]{1,0:T(8,128)S(1)} fusion(f32[32,1024]{1,0:T(8,128)S(1)} %bitcast.108, f32[1,1024,1024]{2,1,0:T(8,128)} %param.6), kind=kOutput, calls=%fused_computation.1 | convolution fusion | flops 402653184 | bytes 4456448 | tf_op jit(solution)/shard_map/dot_general | solution.py:84
  69.6 17.3 %all_to_all.63 = f32[4,32,1024]{2,1,0:T(8,128)S(1)} all-to-all(f32[4,32,1024]{2,1,0:T(8,128)S(1)} %broadcast_in_dim.86), channel_id=1, replica_groups=mesh['island'=16,'row'=4,'col'=4] {'row'}, dimensions={0} | all-to-all | bytes 1048576 | tf_op jit(solution)/shard_map/all_to_all | solution.py:11
  87.2 27.9 %all_to_all.64 = f32[16,1,32,1024]{3,2,1,0:T(8,128)S(1)} all-to-all(f32[16,1,32,1024]{3,2,1,0:T(8,128)S(1)} %broadcast_in_dim.87), channel_id=1, replica_groups=mesh['island'=16,'row'=4,'col'=4] {'island'}, dimensions={0} | all-to-all | bytes 4194304 | tf_op jit(solution)/shard_map/all_to_all | solution.py:11
  115.1 3.8 %bitcast_subtract_fusion = f32[1024,1024]{1,0:T(8,128)S(1)} fusion(f32[1,1024,1024]{2,1,0:T(8,128)S(1)} %copy-done.2, f32[32,1024]{1,0:T(8,128)S(1)} %bitcast.109, f32[32,1024]{1,0:T(8,128)S(1)} %reduce_sum.111, f32[16,1,32,1024]{3,2,1,0:T(8,128)S(1)} %all_to_all.64, s32[]{:T(128)S(6)} %select_n.38), kind=kOutput, calls=%fused_computation | convolution fusion | flops 404783104 | bytes 8781828 | tf_op jit(solution)/shard_map/dot_general | solution.py:87
  120.9 3.9 %fusion.3 = f32[1024,32]{0,1:T(8,128)S(1)} fusion(f32[1024,1024]{1,0:T(8,128)S(1)} %bitcast_subtract_fusion, f32[2,32,1024]{2,1,0:T(8,128)S(1)} %copy-done.3), kind=kOutput, calls=%fused_computation.8 | convolution fusion | flops 402653184 | bytes 4456448 | tf_op jit(solution)/shard_map/dot_general | solution.py:71
  124.9 10.7 %all_to_all.65 = f32[4,32,256]{2,1,0:T(8,128)S(1)} all-to-all(f32[4,32,256]{2,1,0:T(8,128)S(1)} %bitcast.112), channel_id=1, replica_groups=mesh['island'=16,'row'=4,'col'=4] {'col'}, dimensions={0} | all-to-all | bytes 262144 | tf_op jit(solution)/shard_map/all_to_all | solution.py:33
  136.4 3.6 %all-to-all-start.7 = ((f32[16,1,32,256]{3,2,1,0:T(8,128)}), f32[16,1,32,256]{3,2,1,0:T(8,128)S(1)}, u32[]{:S(2)}, u32[]{:S(2)}) async-start(f32[16,1,32,256]{3,2,1,0:T(8,128)} %broadcast_in_dim.88), calls=%async_computation.7 | async-start | bytes 1048576 | tf_op jit(solution)/shard_map/all_to_all | solution.py:11
  142.4 7.8 %all-to-all-done.7 = f32[16,1,32,256]{3,2,1,0:T(8,128)S(1)} async-done(((f32[16,1,32,256]{3,2,1,0:T(8,128)}), f32[16,1,32,256]{3,2,1,0:T(8,128)S(1)}, u32[]{:S(2)}, u32[]{:S(2)}) %all-to-all-start.7) | async-done | bytes 524320 | tf_op jit(solution)/shard_map/all_to_all | solution.py:11
  150.6 14.4 %all_to_all.66 = f32[16,1,1024]{2,1,0:T(1,128)S(1)} all-to-all(f32[16,1,1024]{2,1,0:T(1,128)S(1)} %reshape.58), channel_id=1, replica_groups=mesh['island'=16,'row'=4,'col'=4] {'row','col'}, dimensions={0} | all-to-all | bytes 131072 | tf_op jit(solution)/shard_map/all_to_all | solution.py:11
  166.1 2.9 %cholesky.55 = f32[32,32]{1,0:T(8,128)S(1)} custom-call(f32[32,32]{1,0:T(8,128)S(1)} %fusion.20), custom_call_target="Cholesky" | custom-call | tf_op jit(solution)/shard_map/jit(cholesky)/cholesky | solution.py:51
  170.5 2.4 %custom-call.7 = f32[1,32,32]{1,2,0:T(8,128)S(1)} custom-call(f32[1,32,32]{2,1,0:T(8,128)S(1)} %fusion.18), custom_call_target="InvertDiagBlocksLowerTriangular" | custom-call | tf_op jit(solution)/shard_map/jit(_solve_triangular)/triangular_solve | solution.py:52
  173.2 6.1 %all_to_all.67 = f32[4,32,256]{2,1,0:T(8,128)S(1)} all-to-all(f32[4,32,256]{2,1,0:T(8,128)S(1)} %broadcast_in_dim.92), channel_id=1, replica_groups=mesh['island'=16,'row'=4,'col'=4] {'col'}, dimensions={0} | all-to-all | bytes 262144 | tf_op jit(solution)/shard_map/all_to_all | solution.py:11
  179.3 4.7 %fusion.39 = f32[32,1024]{1,0:T(8,128)S(1)} fusion(f32[32,1024]{1,0:T(8,128)S(1)} %bitcast.106, f32[1024,1024]{1,0:T(8,128)} %copy-done), kind=kOutput, calls=%fused_computation.75 | convolution fusion | flops 402653184 | bytes 4456448 | tf_op jit(solution)/shard_map/dot_general | solution.py:84
  184.1 17.3 %all_to_all.68 = f32[4,32,1024]{2,1,0:T(8,128)S(1)} all-to-all(f32[4,32,1024]{2,1,0:T(8,128)S(1)} %broadcast_in_dim.93), channel_id=1, replica_groups=mesh['island'=16,'row'=4,'col'=4] {'row'}, dimensions={0} | all-to-all | bytes 1048576 | tf_op jit(solution)/shard_map/all_to_all | solution.py:11
  201.7 27.9 %all_to_all.69 = f32[16,1,32,1024]{3,2,1,0:T(8,128)S(1)} all-to-all(f32[16,1,32,1024]{3,2,1,0:T(8,128)S(1)} %broadcast_in_dim.94), channel_id=1, replica_groups=mesh['island'=16,'row'=4,'col'=4] {'island'}, dimensions={0} | all-to-all | bytes 4194304 | tf_op jit(solution)/shard_map/all_to_all | solution.py:11
  229.5 5.2 %subtract_bitcast_fusion = f32[1,1024,1024]{2,1,0:T(8,128)} fusion(f32[1024,1024]{1,0:T(8,128)S(1)} %copy-done.1, f32[32,1024]{1,0:T(8,128)S(1)} %bitcast.107, f32[32,1024]{1,0:T(8,128)S(1)} %reduce_sum.118, f32[16,1,32,1024]{3,2,1,0:T(8,128)S(1)} %all_to_all.69, s32[]{:T(128)S(6)} %select_n.42), kind=kOutput, calls=%fused_computation.3 | convolution fusion | flops 404783104 | bytes 8781828 | tf_op jit(solution)/shard_map/dot_general | solution.py:87
  (56 shorter events, 12.6 us)
Async XLA Ops:
  0.0 21.8 %copy-start.4 = (s32[2,8,2]{1,2,0:T(2,128)S(1)}, s32[2,8,2]{1,2,0:T(2,128)}, u32[]{:S(2)}) copy-start(s32[2,8,2]{1,2,0:T(2,128)} %param.8) | copy-start | bytes 388
  16.2 14.6 %all-to-all-start.1 = ((f32[16,1,32,256]{3,2,1,0:T(8,128)}), f32[16,1,32,256]{3,2,1,0:T(8,128)S(1)}, u32[]{:S(2)}, u32[]{:S(2)}) async-start(f32[16,1,32,256]{3,2,1,0:T(8,128)} %broadcast_in_dim.79), calls=%async_computation.1 | async-start | bytes 1048576 | tf_op jit(solution)/shard_map/all_to_all | solution.py:11
  86.9 28.2 %copy-start.2 = (f32[1,1024,1024]{2,1,0:T(8,128)S(1)}, f32[1,1024,1024]{2,1,0:T(8,128)}, u32[]{:S(2)}) copy-start(f32[1,1024,1024]{2,1,0:T(8,128)} %param.6) | copy-start | bytes 12582916
  115.1 5.8 %copy-start.3 = (f32[2,32,1024]{2,1,0:T(8,128)S(1)}, f32[2,32,1024]{2,1,0:T(8,128)}, u32[]{:S(2)}) copy-start(f32[2,32,1024]{2,1,0:T(8,128)} %param.7) | copy-start | bytes 786436
  118.9 2.0 copy-start
  136.4 13.8 %all-to-all-start.7 = ((f32[16,1,32,256]{3,2,1,0:T(8,128)}), f32[16,1,32,256]{3,2,1,0:T(8,128)S(1)}, u32[]{:S(2)}, u32[]{:S(2)}) async-start(f32[16,1,32,256]{3,2,1,0:T(8,128)} %broadcast_in_dim.88), calls=%async_computation.7 | async-start | bytes 1048576 | tf_op jit(solution)/shard_map/all_to_all | solution.py:11
  201.4 28.1 %copy-start.1 = (f32[1024,1024]{1,0:T(8,128)S(1)}, f32[1024,1024]{1,0:T(8,128)}, u32[]{:S(2)}) copy-start(f32[1024,1024]{1,0:T(8,128)} %copy-done) | copy-start | bytes 12582916
where the time goes:
time: 239 us; the launch traced here: 235 us
  blocking collectives  156 us (65%)
  matrix products  29.2 us (12%)
  other arithmetic  16.8 us (7%)
  waiting for transfers between devices  13.9 us (6%)
  starting transfers between devices  9.19 us (4%)
  local copies, waits for them, and re-layouts  5.67 us (2%)
  between operations  4.09 us (2%)
    all_to_all x8, blocking collectives, copy_for_each(): return lax.all_to_all(copies, axis, split_axis=0, concat_axis=0, tiled=True)  136 us
    all_to_all x2, blocking collectives, sum_at_owner(): lax.all_to_all(blocks, axis, split_axis=0, concat_axis=0, tiled=True)  19.9 us
    all_to_all x2, waiting for transfers between devices, copy_for_each(): return lax.all_to_all(copies, axis, split_axis=0, concat_axis=0, tiled=True)  13.9 us
    dot_general x2, matrix products, shards(): lax.dot_general(base_rows, weight_tile, (((1,), (1,)), ((), ())), precisi...  10 us
    dot_general x2, matrix products, shards(): jnp.dot(left_basis, weight_tile, precision=lax.Precision.HIGHEST)  9.35 us
    all_to_all x2, starting transfers between devices, copy_for_each(): return lax.all_to_all(copies, axis, split_axis=0, concat_axis=0, tiled=True)  9.19 us
    dot_general x2, matrix products, shards(): lax.dot_general(left_basis, right_factor, (((0,), (0,)), ((), ())), preci...  9 us
    another operation x6, other arithmetic, orthonormal(): lower_factor = jnp.linalg.cholesky(gram_matrix)  7.27 us
  transfers between devices with their start and end apart: 2, of which 2 were waited for; matrix products, arithmetic and copies ran while one was open for 1% of the time, Pallas kernels for 0%

commit v1 on v0

v1 whole, which is shorter than its diff:
```python
import jax
import jax.numpy as jnp
from jax import lax
from jax.experimental import pallas as pl
from jax.experimental.pallas import tpu as pltpu
from jax.sharding import PartitionSpec as P

MESH = pl.DeviceIdType.MESH
RANK = 32
WIDTH = 1024
TILES = 32
BLOCKS = WIDTH // 128
ISLANDS = 16
SIDE = 4
PEERS = ISLANDS * SIDE
HIGHEST = lax.Precision.HIGHEST


def halves(array):
    high = array.astype(jnp.bfloat16)
    low = (array - high.astype(jnp.float32)).astype(jnp.bfloat16)
    return high, low


def device(island, row, col):
    return {"island": island, "row": row, "col": col}


def exact_dot(left, right, dims):
    return lax.dot_general(
        left, right, (dims, ((), ())), precision=HIGHEST, preferred_element_type=jnp.float32
    )


def inverse(gram):
    rows = lax.broadcasted_iota(jnp.int32, (RANK, RANK), 0)
    cols = lax.broadcasted_iota(jnp.int32, (RANK, RANK), 1)

    def step(pivot, matrix):
        pivot_row = jnp.sum(jnp.where(rows == pivot, matrix, 0.0), axis=0, keepdims=True)
        pivot_col = jnp.sum(jnp.where(cols == pivot, matrix, 0.0), axis=1, keepdims=True)
        corner = jnp.sum(jnp.where(cols[:1] == pivot, pivot_row, 0.0), axis=1, keepdims=True)
        scale = 1.0 / corner
        plain = matrix - (pivot_col * scale) * pivot_row
        in_row, in_col = rows == pivot, cols == pivot
        edge = jnp.where(in_row, pivot_row * scale, pivot_col * scale)
        swept = jnp.where(in_row | in_col, edge, plain)
        return jnp.where(in_row & in_col, -scale, swept)

    return -lax.fori_loop(0, RANK, step, gram)


def exchange_kernel(
    weights_ref, bases_ref, pairs_ref, left_ref, right_ref,
    plain, high_ref, low_ref, partner, sent, arrived, summed, combined, given,
    gram_sent, gram_got, load_sem, send_sem, own_sem, back_sem, get_sem, gram_send, gram_sem,
):
    island, row, col = (lax.axis_index(name) for name in ("island", "row", "col"))
    side, core = col // 2, col % 2
    other = (1 - side) * 2 + core

    loads = []
    for part in range(4):
        rows = pl.ds(part * 256, 256)
        load = pltpu.make_async_copy(
            weights_ref.at[0, rows, :], plain.at[rows, :], load_sem.at[part]
        )
        load.start()
        loads.append(load)

    barrier = pltpu.get_barrier_semaphore()

    def greet(index, carry):
        k, m = index // SIDE, index % SIDE

        @pl.when((k != island) | (m != col))
        def _():
            pl.semaphore_signal(barrier, inc=1, device_id=device(k, row, m), device_id_type=MESH)

        pl.semaphore_signal(barrier, inc=1, device_id=device(k, m, other), device_id_type=MESH)
        return carry

    lax.fori_loop(0, PEERS, greet, 0)
    for step in range(1, SIDE):
        pl.semaphore_signal(
            barrier, inc=1, device_id=device(island, (row + step) % SIDE, col), device_id_type=MESH
        )

    def find(index, carry):
        for matching in range(2):
            found = jnp.int32(0)
            for pair in range(ISLANDS // 2):
                first, second = pairs_ref[matching, pair, 0], pairs_ref[matching, pair, 1]
                found += jnp.where(first == index, second, 0) + jnp.where(second == index, first, 0)
            partner[matching, index] = found
        return carry

    lax.fori_loop(0, ISLANDS, find, 0)

    bases = bases_ref[...].reshape(2 * RANK, WIDTH)
    base_high, base_low = halves(bases)
    base_stack = jnp.concatenate([base_high, base_low], axis=0)
    contract_last = ((1,), (1,))
    contract_first = ((0,), (0,))
    raw_parts = []
    for part in range(4):
        loads[part].wait()
        rows = pl.ds(part * 256, 256)
        high, low = halves(plain[rows, :])
        high_ref[rows, :] = high
        low_ref[rows, :] = low
        wide = lax.dot_general(
            base_stack, high, (contract_last, ((), ())), preferred_element_type=jnp.float32
        )
        fine = lax.dot_general(
            base_high, low, (contract_last, ((), ())), preferred_element_type=jnp.float32
        )
        terms = wide[: 2 * RANK] + (wide[2 * RANK :] + fine)
        for a in range(4):
            for b in range(2):
                sent[0, a * BLOCKS + part * 2 + b] = terms[a * 8 : a * 8 + 8, b * 128 : b * 128 + 128]
        raw_parts.append(terms[RANK:])
    raw_terms = jnp.concatenate(raw_parts, axis=1)

    pl.semaphore_wait(barrier, 2 * PEERS - 1 + SIDE - 1)

    row_owner = core == island % 2
    row_tile = island * 2 + side
    col_owner = row % 2 == (island + core) % 2
    col_tile = island * 2 + row // 2

    def sized(ref, send, recv):
        return pltpu.make_async_remote_copy(
            ref, ref, send, recv, device_id=device(island, row, other), device_id_type=MESH
        )

    def combine(phase, matching, sign):
        for k in range(ISLANDS):
            summed[k] = (arrived[phase, k * 4] + arrived[phase, k * 4 + 1]) + (
                arrived[phase, k * 4 + 2] + arrived[phase, k * 4 + 3]
            )
        for k in range(ISLANDS):
            combined[phase, k] = summed[k] + sign * summed[partner[matching, k]]

    def over_columns(phase, matching):
        def send(tile, carry):
            k = tile // 2
            m = (tile % 2) * 2 + k % 2

            @pl.when((k != island) | (m != col))
            def _():
                pltpu.make_async_remote_copy(
                    sent.at[phase, tile], arrived.at[phase, island * 4 + col],
                    send_sem.at[phase], own_sem.at[phase],
                    device_id=device(k, row, m), device_id_type=MESH,
                ).start()

            return carry

        lax.fori_loop(0, TILES, send, 0)

        @pl.when(row_owner)
        def _():
            arrived[phase, island * 4 + col] = sent[phase, row_tile]
            sized(arrived.at[phase, pl.ds(0, PEERS - 1)], send_sem.at[phase], own_sem.at[phase]).wait_recv()
            combine(phase, matching, -1.0)

            def give(index, carry):
                k, m = index // SIDE, index % SIDE

                @pl.when((k != island) | (m != col))
                def _():
                    pltpu.make_async_remote_copy(
                        combined.at[phase, k], given.at[phase, row_tile],
                        back_sem.at[phase], get_sem.at[phase],
                        device_id=device(k, row, m), device_id_type=MESH,
                    ).start()

                return carry

            lax.fori_loop(0, PEERS, give, 0)
            given[phase, row_tile] = combined[phase, island]
            sized(given.at[phase, pl.ds(0, TILES - 1)], send_sem.at[phase], get_sem.at[phase]).wait_recv()

        @pl.when(jnp.logical_not(row_owner))
        def _():
            sized(given.at[phase], send_sem.at[phase], get_sem.at[phase]).wait_recv()

    def send_over_rows(phase):
        def send(tile, carry):
            k = tile // 2
            m = (tile % 2) * 2 + (k + core) % 2
            pltpu.make_async_remote_copy(
                sent.at[phase, tile], arrived.at[phase, island * 4 + row],
                send_sem.at[phase], own_sem.at[phase],
                device_id=device(k, m, other), device_id_type=MESH,
            ).start()
            return carry

        lax.fori_loop(0, TILES, send, 0)

    def own_over_rows(phase, matching):
        @pl.when(col_owner)
        def _():
            sized(arrived.at[phase], send_sem.at[phase], own_sem.at[phase]).wait_recv()
            combine(phase, matching, 1.0)

            def give(index, carry):
                k, m = index // SIDE, index % SIDE
                pltpu.make_async_remote_copy(
                    combined.at[phase, k], given.at[phase, col_tile],
                    back_sem.at[phase], get_sem.at[phase],
                    device_id=device(k, m, other), device_id_type=MESH,
                ).start()
                return carry

            lax.fori_loop(0, PEERS, give, 0)

    def finish_over_rows(phase):
        sized(given.at[phase], send_sem.at[phase], get_sem.at[phase]).wait_recv()

    def whole(phase):
        return jnp.concatenate(
            [
                jnp.concatenate([given[phase, a * BLOCKS + b] for b in range(BLOCKS)], axis=1)
                for a in range(4)
            ],
            axis=0,
        )

    def put(phase, value, part):
        for a in range(4):
            for b in range(2):
                sent[phase, a * BLOCKS + part * 2 + b] = value[a * 8 : a * 8 + 8, b * 128 : b * 128 + 128]

    def gram_start(matching, factor):
        gram = exact_dot(factor, factor, contract_last)
        gram_sent[matching] = jnp.concatenate([gram, jnp.zeros((RANK, 128 - RANK), jnp.float32)], axis=1)
        gram_got[matching, row] = gram_sent[matching]
        for step in range(1, SIDE):
            pltpu.make_async_remote_copy(
                gram_sent.at[matching], gram_got.at[matching, row],
                gram_send.at[matching], gram_sem.at[matching],
                device_id=device(island, (row + step) % SIDE, col), device_id_type=MESH,
            ).start()

    def gram_finish(matching):
        sized(gram_got.at[matching, pl.ds(0, SIDE - 1)], gram_send.at[matching], gram_sem.at[matching]).wait_recv()
        total = (gram_got[matching, 0] + gram_got[matching, 1]) + (gram_got[matching, 2] + gram_got[matching, 3])
        return inverse(total[:, :RANK])

    lefts, rights = [], []
    for matching in range(2):
        first, second = matching * 2, matching * 2 + 1
        if matching == 1:
            mix = exact_dot(bases_ref[1], rights[0], contract_last)
            terms = raw_terms - exact_dot(mix, lefts[0], ((1,), (0,)))
            for part in range(4):
                put(first, terms[:, part * 256 : part * 256 + 256], part)
        over_columns(first, matching)
        factor = whole(first)
        gram_start(matching, factor)
        factor_high, factor_low = halves(factor)
        factor_stack = jnp.concatenate([factor_high, factor_low], axis=0)
        if matching == 1:
            seen = exact_dot(factor, lefts[0], contract_last)
            drop = exact_dot(seen, rights[0], ((1,), (0,)))
        for part in range(4):
            cols = pl.ds(part * 256, 256)
            wide = jnp.dot(factor_stack, high_ref[:, cols], preferred_element_type=jnp.float32)
            fine = jnp.dot(factor_high, low_ref[:, cols], preferred_element_type=jnp.float32)
            terms = wide[:RANK] + (wide[RANK:] + fine)
            if matching == 1:
                terms = terms - drop[:, part * 256 : part * 256 + 256]
            put(second, terms, part)
        send_over_rows(second)
        left = 0.5 * exact_dot(gram_finish(matching), factor, ((1,), (0,)))
        own_over_rows(second, matching)
        finish_over_rows(second)
        lefts.append(left)
        rights.append(whole(second))
        left_ref[pl.ds(matching * RANK, RANK), :] = left
        right_ref[pl.ds(matching * RANK, RANK), :] = rights[-1]

    for matching in range(2):
        first, second = matching * 2, matching * 2 + 1
        sized(gram_got.at[matching, pl.ds(0, SIDE - 1)], gram_send.at[matching], gram_sem.at[matching]).wait_send()
        sized(sent.at[second], send_sem.at[second], own_sem.at[second]).wait_send()

        @pl.when(row_owner)
        def _():
            sized(sent.at[first, pl.ds(0, TILES - 1)], send_sem.at[first], own_sem.at[first]).wait_send()
            sized(arrived.at[first, pl.ds(0, PEERS - 1)], back_sem.at[first], own_sem.at[first]).wait_send()

        @pl.when(jnp.logical_not(row_owner))
        def _():
            sized(sent.at[first], send_sem.at[first], own_sem.at[first]).wait_send()

        @pl.when(col_owner)
        def _():
            sized(arrived.at[second], back_sem.at[second], own_sem.at[second]).wait_send()


def update_kernel(weights_ref, left_ref, right_ref, out_ref, right_stack):
    @pl.when(pl.program_id(0) == 0)
    def _():
        high, low = halves(right_ref[...])
        right_stack[...] = jnp.concatenate([high, low, high], axis=0)

    high, low = halves(left_ref[...])
    left_stack = jnp.concatenate([high, high, low], axis=0)
    correction = lax.dot_general(
        left_stack, right_stack[...], (((0,), (0,)), ((), ())), preferred_element_type=jnp.float32
    )
    out_ref[0] = weights_ref[0] - correction


def shards(weights, bases, pairs):
    vmem = pl.BlockSpec(memory_space=pltpu.VMEM)
    factors = jax.ShapeDtypeStruct((2 * RANK, WIDTH), jnp.float32)
    left, right = pl.pallas_call(
        exchange_kernel,
        out_shape=(factors, factors),
        in_specs=[pl.BlockSpec(memory_space=pl.ANY), vmem, pl.BlockSpec(memory_space=pltpu.SMEM)],
        out_specs=(vmem, vmem),
        scratch_shapes=[
            pltpu.VMEM((WIDTH, WIDTH), jnp.float32),
            pltpu.VMEM((WIDTH, WIDTH), jnp.bfloat16),
            pltpu.VMEM((WIDTH, WIDTH), jnp.bfloat16),
            pltpu.SMEM((2, ISLANDS), jnp.int32),
            pltpu.VMEM((4, TILES, 8, 128), jnp.float32),
            pltpu.VMEM((4, PEERS, 8, 128), jnp.float32),
            pltpu.VMEM((ISLANDS, 8, 128), jnp.float32),
            pltpu.VMEM((4, ISLANDS, 8, 128), jnp.float32),
            pltpu.VMEM((4, TILES, 8, 128), jnp.float32),
            pltpu.VMEM((2, RANK, 128), jnp.float32),
            pltpu.VMEM((2, SIDE, RANK, 128), jnp.float32),
            pltpu.SemaphoreType.DMA((4,)),
            pltpu.SemaphoreType.DMA((4,)),
            pltpu.SemaphoreType.DMA((4,)),
            pltpu.SemaphoreType.DMA((4,)),
            pltpu.SemaphoreType.DMA((4,)),
            pltpu.SemaphoreType.DMA((2,)),
            pltpu.SemaphoreType.DMA((2,)),
        ],
        compiler_params=pltpu.CompilerParams(
            collective_id=0, has_side_effects=True, vmem_limit_bytes=40 * 2**20
        ),
        name="exchange",
    )(weights, bases, pairs)
    rows = 256
    return pl.pallas_call(
        update_kernel,
        out_shape=jax.ShapeDtypeStruct(weights.shape, jnp.float32),
        grid=(WIDTH // rows,),
        in_specs=[
            pl.BlockSpec((1, rows, WIDTH), lambda i: (0, i, 0)),
            pl.BlockSpec((2 * RANK, rows), lambda i: (0, i)),
            pl.BlockSpec((2 * RANK, WIDTH), lambda i: (0, 0)),
        ],
        out_specs=pl.BlockSpec((1, rows, WIDTH), lambda i: (0, i, 0)),
        scratch_shapes=[pltpu.VMEM((6 * RANK, WIDTH), jnp.bfloat16)],
        name="update",
    )(weights, left, right)


def solution(mesh):
    in_specs = (P("island", "row", "col"), P(None, None, "col"), P())
    out_specs = P("island", "row", "col")
    return jax.shard_map(shards, mesh=mesh, in_specs=in_specs, out_specs=out_specs, check_vma=False)
```

time: 239 us -> 82.9 us (0.35); the launches traced: 235 us -> 81.7 us
  blocking collectives: 156 us -> 0 us
  Pallas kernels: 0 us -> 76.4 us
  matrix products: 29.2 us -> 0 us
  other arithmetic: 16.8 us -> 0 us
  waiting for transfers between devices: 13.9 us -> 0 us
  starting transfers between devices: 9.19 us -> 0 us
  between operations: 4.09 us -> 0.02 us
    all_to_all x10 -> x0, blocking collectives: 156 us -> none  [the longest x8 136 us: copy_for_each(): return lax.all_to_all(copies, axis, split_axis=0, concat_axis=0, tiled=True)]
    pallas_call x0 -> x2, Pallas kernels: none -> 76.4 us  [the longest x1 70.8 us: shards(): pl.pallas_call(exchange_kernel, out_shape=(factors, factors), in_specs=[p...]
    dot_general x8 -> x0, matrix products: 28.7 us -> none  [the longest x2 10 us: shards(): lax.dot_general(base_rows, weight_tile, (((1,), (1,)), ((), ())), precisi...]
    all_to_all x2 -> x0, waiting for transfers between devices: 13.9 us -> none  [copy_for_each(): return lax.all_to_all(copies, axis, split_axis=0, concat_axis=0, tiled=True)]
    another operation x10 -> x0, other arithmetic: 13.5 us -> none  [the longest x6 7.27 us: orthonormal(): lower_factor = jnp.linalg.cholesky(gram_matrix)]
    all_to_all x2 -> x0, starting transfers between devices: 9.19 us -> none  [copy_for_each(): return lax.all_to_all(copies, axis, split_axis=0, concat_axis=0, tiled=True)]
    unnamed x14 -> x9, local copies, waits for them, and re-layouts: 2.58 us -> 5.28 us
  transfers between devices with their start and end apart: 2 -> 0, of which waited for: 2 -> 0; matrix products, arithmetic and copies ran while one was open for 1% -> 0% of each run, Pallas kernels for 0% -> 0%
where the time goes in v1:
time: 82.9 us; the launch traced here: 81.7 us
  Pallas kernels  76.4 us (92%)
  local copies, waits for them, and re-layouts  5.28 us (6%)
    pallas_call x1, Pallas kernels, shards(): pl.pallas_call(exchange_kernel, out_shape=(factors, factors), in_specs=[p...  70.8 us
    pallas_call x1, Pallas kernels, shards(): pl.pallas_call(update_kernel, out_shape=jax.ShapeDtypeStruct(weights.shap...  5.64 us
    unnamed x9, local copies, waits for them, and re-layouts  5.28 us

profile of v1, /device:TPU:1, one launch (start us, length us, event | category | flops | bytes accessed | tf_op | source)
XLA Modules:
  0.0 81.7 jit_solution(4136258314200485758)
XLA Ops:
  0.0 0.8 copy.4.pairs_ref
  0.8 0.0 copy-start
  0.8 2.2 %copy-done = f32[1,1024,1024]{2,1,0:T(8,128)S(1)} copy-done((f32[1,1024,1024]{2,1,0:T(8,128)S(1)}, f32[1,1024,1024]{2,1,0:T(8,128)}, u32[]{:S(2)}) %copy-start) | copy-done | bytes 4194328
  3.0 0.0 copy-start.1
  3.0 0.9 %copy-done.1 = f32[2,32,1024]{2,1,0:T(8,128)S(1)} copy-done((f32[2,32,1024]{2,1,0:T(8,128)S(1)}, f32[2,32,1024]{2,1,0:T(8,128)}, u32[]{:S(2)}) %copy-start.1) | copy-done | bytes 262168
  3.9 70.8 %exchange.1 = (f32[64,1024]{1,0:T(8,128)S(1)}, f32[64,1024]{1,0:T(8,128)S(1)}) custom-call(f32[1,1024,1024]{2,1,0:T(8,128)S(1)} %copy-done, f32[2,32,1024]{2,1,0:T(8,128)S(1)} %copy-done.1, s32[2,8,2]{2,1,0:T(8,128)S(1)} %copy.4.pairs_ref), custom_call_target="tpu_custom_call" | custom-call | tf_op jit(solution)/shard_map/exchange/pallas_call | solution.py:321
  74.7 0.0 copy-start.2
  74.7 0.7 copy-done.2
  75.4 0.0 copy-start.3
  75.4 0.7 copy-done.3
  76.1 5.6 %update.1 = f32[1,1024,1024]{2,1,0:T(8,128)} custom-call(f32[1,1024,1024]{2,1,0:T(8,128)} %weights_ref.3, f32[64,1024]{1,0:T(8,128)} %copy-done.2, f32[64,1024]{1,0:T(8,128)} %copy-done.3), custom_call_target="tpu_custom_call" | custom-call | tf_op jit(solution)/shard_map/update/pallas_call | solution.py:352
Async XLA Ops:
  0.8 2.2 %copy-start = (f32[1,1024,1024]{2,1,0:T(8,128)S(1)}, f32[1,1024,1024]{2,1,0:T(8,128)}, u32[]{:S(2)}) copy-start(f32[1,1024,1024]{2,1,0:T(8,128)} %weights_ref.3) | copy-start | bytes 12582916
  3.0 0.9 %copy-start.1 = (f32[2,32,1024]{2,1,0:T(8,128)S(1)}, f32[2,32,1024]{2,1,0:T(8,128)}, u32[]{:S(2)}) copy-start(f32[2,32,1024]{2,1,0:T(8,128)} %bases_ref.1) | copy-start | bytes 786436
  74.7 0.7 copy-start.2
  75.4 0.7 copy-start.3

commit v2 on v1

v2 whole, which is shorter than its diff:
```python
import jax
import jax.numpy as jnp
from jax import lax
from jax.experimental import pallas as pl
from jax.experimental.pallas import tpu as pltpu
from jax.sharding import PartitionSpec as P

MESH = pl.DeviceIdType.MESH
RANK = 32
WIDTH = 1024
TILES = 32
BLOCKS = WIDTH // 128
ISLANDS = 16
SIDE = 4
PEERS = ISLANDS * SIDE
HIGHEST = lax.Precision.HIGHEST
LAST = (((1,), (1,)), ((), ()))
FIRST = (((0,), (0,)), ((), ()))
PLAIN = (((1,), (0,)), ((), ()))


def halves(array):
    high = array.astype(jnp.bfloat16)
    low = (array - high.astype(jnp.float32)).astype(jnp.bfloat16)
    return high, low


def device(island, row, col):
    return {"island": island, "row": row, "col": col}


def exact_dot(left, right, dims):
    return lax.dot_general(left, right, dims, precision=HIGHEST, preferred_element_type=jnp.float32)


def fast_dot(left, right, dims):
    return lax.dot_general(left, right, dims, preferred_element_type=jnp.float32)


def stack(*rows):
    return jnp.concatenate(rows, axis=0)


def eliminate(matrix, double):
    rows = lax.broadcasted_iota(jnp.int32, (RANK, 128), 0)
    lanes = lax.broadcasted_iota(jnp.int32, (1, 128), 1)
    for pivot in range(RANK):
        factor = matrix[:, pivot : pivot + 1]
        here = lanes == pivot
        if double:
            factor = jnp.where(lanes < 64, factor, matrix[:, 64 + pivot : 65 + pivot])
            here = here | (lanes == 64 + pivot)
        else:
            factor = jnp.broadcast_to(factor, (RANK, 128))
        scaled = jnp.where(here, 1.0, matrix[pivot : pivot + 1]) / factor[pivot : pivot + 1]
        rest = jnp.where(here, 0.0, matrix) - factor * scaled
        matrix = jnp.where(rows == pivot, scaled, rest)
    return matrix


def exchange_kernel(
    weights_ref, bases_ref, pairs_ref, left_ref, right_ref,
    plain, high_ref, low_ref, bases_in, partner, sent, arrived, summed,
    near_out, wide_out, late_out, sums_out, last_out, near_in, wide_in, late_in, sums_in, last_in,
    gram_sent, gram_got,
    load_sem, send_sem, own_sem, back_sem, get_sem, gram_send, gram_sem, ready_sem,
):
    island, row, col = (lax.axis_index(name) for name in ("island", "row", "col"))
    side, core = col // 2, col % 2
    other = (1 - side) * 2 + core

    base_load = pltpu.make_async_copy(bases_ref, bases_in, load_sem.at[4])
    base_load.start()
    loads = []
    for part in range(4):
        rows = pl.ds(part * 256, 256)
        load = pltpu.make_async_copy(
            weights_ref.at[0, rows, :], plain.at[rows, :], load_sem.at[part]
        )
        load.start()
        loads.append(load)

    barrier = pltpu.get_barrier_semaphore()

    def greet(index, carry):
        k, m = index // SIDE, index % SIDE

        @pl.when((k != island) | (m != col))
        def _():
            pl.semaphore_signal(barrier, inc=1, device_id=device(k, row, m), device_id_type=MESH)

        return carry

    lax.fori_loop(0, PEERS, greet, 0)
    for step in range(1, SIDE):
        pl.semaphore_signal(
            barrier, inc=1, device_id=device(island, (row + step) % SIDE, col), device_id_type=MESH
        )

    def find(index, carry):
        for matching in range(2):
            found = jnp.int32(0)
            for pair in range(ISLANDS // 2):
                first, second = pairs_ref[matching, 0, pair], pairs_ref[matching, 1, pair]
                found += jnp.where(first == index, second, 0) + jnp.where(second == index, first, 0)
            partner[matching, index] = found
        return carry

    lax.fori_loop(0, ISLANDS, find, 0)

    base_load.wait()
    base_high, base_low = halves(bases_in[...].reshape(2 * RANK, WIDTH))
    base_stack = stack(base_high, base_low)

    def put(flow, value, part):
        for a in range(4):
            for b in range(2):
                sent[flow, a * BLOCKS + part * 2 + b] = value[a * 8 : a * 8 + 8, b * 128 : b * 128 + 128]

    for part in range(4):
        loads[part].wait()
        rows = pl.ds(part * 256, 256)
        high, low = halves(plain[rows, :])
        high_ref[rows, :] = high
        low_ref[rows, :] = low
        wide = fast_dot(base_stack, high, LAST)
        fine = fast_dot(base_high, low, LAST)
        terms = wide[: 2 * RANK] + (wide[2 * RANK :] + fine)
        put(0, terms[:RANK], part)
        put(1, terms[RANK:], part)

    pl.semaphore_wait(barrier, PEERS - 1 + SIDE - 1)
    for step in range(1, SIDE):
        pl.semaphore_signal(
            ready_sem, inc=1, device_id=device(island, (row + step) % SIDE, col), device_id_type=MESH
        )

    row_owner = core == island % 2
    row_tile = island * 2 + side
    col_owner = row % 2 == (island + core) % 2
    col_tile = island * 2 + row // 2

    def sized(ref, send, recv):
        return pltpu.make_async_remote_copy(
            ref, ref, send, recv, device_id=device(island, row, other), device_id_type=MESH
        )

    def add_up(flow, slot):
        for k in range(ISLANDS):
            summed[slot, k] = (arrived[flow, k * 4] + arrived[flow, k * 4 + 1]) + (
                arrived[flow, k * 4 + 2] + arrived[flow, k * 4 + 3]
            )

    def send_over_columns(flow):
        def send(index, carry):
            tile = (index + 2 * island) % TILES
            k = tile // 2
            m = (tile % 2) * 2 + k % 2

            @pl.when((k != island) | (m != col))
            def _():
                pltpu.make_async_remote_copy(
                    sent.at[flow, tile], arrived.at[flow, island * 4 + col],
                    send_sem.at[flow], own_sem.at[flow],
                    device_id=device(k, row, m), device_id_type=MESH,
                ).start()

            return carry

        lax.fori_loop(0, TILES, send, 0)

    def owned_over_columns(flow):
        arrived[flow, island * 4 + col] = sent[flow, row_tile]
        sized(arrived.at[flow, pl.ds(0, PEERS - 1)], send_sem.at[flow], own_sem.at[flow]).wait_recv()
        add_up(flow, flow)

    def give_over_columns(flow, out, into):
        def give(index, carry):
            k, m = (index // SIDE + island) % ISLANDS, index % SIDE

            @pl.when((k != island) | (m != col))
            def _():
                pltpu.make_async_remote_copy(
                    out.at[k], into.at[row_tile], back_sem.at[flow], get_sem.at[flow],
                    device_id=device(k, row, m), device_id_type=MESH,
                ).start()

            return carry

        lax.fori_loop(0, PEERS, give, 0)
        into[row_tile] = out[island]

    def get_over_columns(flow, into):
        @pl.when(row_owner)
        def _():
            sized(into.at[pl.ds(0, TILES - 1)], back_sem.at[flow], get_sem.at[flow]).wait_recv()

        @pl.when(jnp.logical_not(row_owner))
        def _():
            sized(into, back_sem.at[flow], get_sem.at[flow]).wait_recv()

    def send_over_rows(flow):
        def send(index, carry):
            tile = (index + 2 * island) % TILES
            k = tile // 2
            m = (tile % 2) * 2 + (k + core) % 2
            pltpu.make_async_remote_copy(
                sent.at[flow, tile], arrived.at[flow, island * 4 + row],
                send_sem.at[flow], own_sem.at[flow],
                device_id=device(k, m, other), device_id_type=MESH,
            ).start()
            return carry

        lax.fori_loop(0, TILES, send, 0)

    def owned_over_rows(flow):
        sized(arrived.at[flow], send_sem.at[flow], own_sem.at[flow]).wait_recv()
        add_up(flow, flow - 2)

    def give_over_rows(flow, out, into):
        def give(index, carry):
            k, m = (index // SIDE + island) % ISLANDS, index % SIDE
            pltpu.make_async_remote_copy(
                out.at[k], into.at[col_tile], back_sem.at[flow], get_sem.at[flow],
                device_id=device(k, m, other), device_id_type=MESH,
            ).start()
            return carry

        lax.fori_loop(0, PEERS, give, 0)

    def whole(ref, which):
        return stack(
            *(
                jnp.concatenate([ref[a * BLOCKS + b, which] for b in range(BLOCKS)], axis=1)
                for a in range(4)
            )
        )

    def gram_start(slot, gram):
        gram_sent[slot] = gram
        gram_got[slot, row] = gram
        for step in range(1, SIDE):
            pltpu.make_async_remote_copy(
                gram_sent.at[slot], gram_got.at[slot, row], gram_send.at[slot], gram_sem.at[slot],
                device_id=device(island, (row + step) % SIDE, col), device_id_type=MESH,
            ).start()

    def gram_finish(slot):
        sized(gram_got.at[slot, pl.ds(0, SIDE - 1)], gram_send.at[slot], gram_sem.at[slot]).wait_recv()
        return (gram_got[slot, 0] + gram_got[slot, 1]) + (gram_got[slot, 2] + gram_got[slot, 3])

    def times_weights(high, low, count, use):
        both = stack(high, low)
        for part in range(4):
            cols = pl.ds(part * 256, 256)
            wide = fast_dot(both, high_ref[:, cols], PLAIN)
            fine = fast_dot(high, low_ref[:, cols], PLAIN)
            use(wide[:count] + (wide[count:] + fine), part)

    send_over_columns(0)
    send_over_columns(1)

    @pl.when(row_owner)
    def _():
        owned_over_columns(0)
        for k in range(ISLANDS):
            near_out[k, 0] = summed[0, k] - summed[0, partner[0, k]]
        give_over_columns(0, near_out, near_in)
        owned_over_columns(1)
        for k in range(ISLANDS):
            wide_out[k, 0] = near_out[partner[1, k], 0]
            wide_out[k, 1] = summed[1, k] - summed[1, partner[0, k]]
            late_out[k, 0] = summed[1, k] - summed[1, partner[1, k]]
        for k in range(ISLANDS):
            wide_out[k, 2] = wide_out[partner[1, k], 1]
        give_over_columns(1, wide_out, wide_in)
        give_over_columns(2, late_out, late_in)

    get_over_columns(0, near_in)
    near = whole(near_in, 0)
    near_high, near_low = halves(near)
    products = []

    def first_use(value, part):
        put(2, value, part)
        products.append(value)

    times_weights(near_high, near_low, RANK, first_use)
    pl.semaphore_wait(ready_sem, SIDE - 1)
    send_over_rows(2)
    near_product = jnp.concatenate(products, axis=1)

    get_over_columns(1, wide_in)
    far = whole(wide_in, 0)
    far_high, far_low = halves(far)
    near_cross_high, near_cross_low = halves(whole(wide_in, 1))
    far_cross_high, far_cross_low = halves(whole(wide_in, 2))
    lanes = lax.broadcasted_iota(jnp.int32, (RANK, 128), 1)
    block = fast_dot(
        stack(near_high, far_high, near_low, far_low),
        stack(
            near_high, near_cross_high, far_high, far_cross_high,
            near_low, near_cross_low, far_low, far_cross_low,
        ),
        LAST,
    )
    block = block[:64, :128] + (block[:64, 128:] + block[64:, :128])
    gram_start(0, jnp.where(lanes < 64, block[:RANK], block[RANK:]))

    get_over_columns(2, late_in)
    late = whole(late_in, 0)
    late_high, late_low = halves(late)
    later = []
    times_weights(
        stack(late_high, far_high), stack(late_low, far_low), 2 * RANK,
        lambda value, part: later.append(value),
    )
    later = jnp.concatenate(later, axis=1)
    product_high, product_low = halves(stack(near_product, later[RANK:]))

    solved = eliminate(gram_finish(0), True)
    near_inverse, far_inverse = solved[:, :32], solved[:, 64:96]
    mixing = 0.5 * stack(-solved[:, 32:64], solved[:, 96:128])
    mixing_high, mixing_low = halves(mixing)

    def mixed(high, low):
        return fast_dot(mixing_high, high, FIRST) + (
            fast_dot(mixing_high, low, FIRST) + fast_dot(mixing_low, high, FIRST)
        )

    terms = later[:RANK] + mixed(product_high, product_low)
    for part in range(4):
        put(3, terms[:, part * 256 : part * 256 + 256], part)
    send_over_rows(3)

    factor = late + mixed(stack(near_high, far_high), stack(near_low, far_low))
    factor_high, factor_low = halves(factor)
    nothing = jnp.zeros((RANK, WIDTH), jnp.bfloat16)
    block = fast_dot(
        stack(factor_high, factor_low),
        stack(
            factor_high, near_high, far_high, nothing,
            factor_low, near_low, far_low, nothing,
        ),
        LAST,
    )
    gram_start(1, block[:RANK, :128] + (block[:RANK, 128:] + block[RANK:, :128]))

    @pl.when(col_owner)
    def _():
        owned_over_rows(2)
        for k in range(ISLANDS):
            sums_out[k, 0] = summed[0, k] + summed[0, partner[0, k]]
        for k in range(ISLANDS):
            sums_out[k, 1] = sums_out[partner[1, k], 0]
        give_over_rows(3, sums_out, sums_in)

    left_ref[:RANK, :] = 0.5 * exact_dot(near_inverse, near, PLAIN)

    @pl.when(col_owner)
    def _():
        owned_over_rows(3)
        for k in range(ISLANDS):
            last_out[k, 0] = summed[1, k] + summed[1, partner[1, k]]
        give_over_rows(4, last_out, last_in)

    crossed = gram_finish(1)
    left_ref[RANK:, :] = 0.5 * exact_dot(eliminate(crossed, False)[:, :32], factor, PLAIN)
    near_change = -0.5 * exact_dot(crossed[:, 32:64], near_inverse, PLAIN)
    far_change = 0.5 * exact_dot(crossed[:, 64:96], far_inverse, PLAIN)
    sized(sums_in, back_sem.at[3], get_sem.at[3]).wait_recv()
    near_sums = whole(sums_in, 0)
    right_ref[:RANK, :] = near_sums
    change = exact_dot(
        jnp.concatenate([near_change, far_change], axis=1), stack(near_sums, whole(sums_in, 1)), PLAIN
    )
    sized(last_in, back_sem.at[4], get_sem.at[4]).wait_recv()
    right_ref[RANK:, :] = whole(last_in, 0) + change

    for slot in range(2):
        sized(gram_got.at[slot, pl.ds(0, SIDE - 1)], gram_send.at[slot], gram_sem.at[slot]).wait_send()
        sized(sent.at[2 + slot], send_sem.at[2 + slot], own_sem.at[2 + slot]).wait_send()

    @pl.when(row_owner)
    def _():
        for flow in range(2):
            sized(sent.at[flow, pl.ds(0, TILES - 1)], send_sem.at[flow], own_sem.at[flow]).wait_send()
        for flow, count in ((0, 1), (1, 3), (2, 1)):
            sized(
                arrived.at[pl.ds(0, count), pl.ds(0, PEERS - 1)], back_sem.at[flow], get_sem.at[flow]
            ).wait_send()

    @pl.when(jnp.logical_not(row_owner))
    def _():
        for flow in range(2):
            sized(sent.at[flow], send_sem.at[flow], own_sem.at[flow]).wait_send()

    @pl.when(col_owner)
    def _():
        for flow, count in ((3, 2), (4, 1)):
            sized(arrived.at[pl.ds(0, count)], back_sem.at[flow], get_sem.at[flow]).wait_send()


def update_kernel(weights_ref, left_ref, right_ref, out_ref, right_stack):
    rows = out_ref.shape[1]
    step = pl.program_id(0)

    @pl.when(step == 0)
    def _():
        high, low = halves(right_ref[...])
        right_stack[...] = stack(high, low, high)

    high, low = halves(left_ref[:, pl.ds(pl.multiple_of(step * rows, rows), rows)])
    out_ref[0] = weights_ref[0] - fast_dot(stack(high, high, low), right_stack[...], FIRST)


def shards(weights, bases, pairs):
    vmem = pl.BlockSpec(memory_space=pltpu.VMEM)
    anywhere = pl.BlockSpec(memory_space=pl.ANY)
    factors = jax.ShapeDtypeStruct((2 * RANK, WIDTH), jnp.float32)

    def tiles(*lead):
        return pltpu.VMEM((*lead, 8, 128), jnp.float32)

    dma = pltpu.SemaphoreType.DMA
    left, right = pl.pallas_call(
        exchange_kernel,
        out_shape=(factors, factors),
        in_specs=[anywhere, anywhere, pl.BlockSpec(memory_space=pltpu.SMEM)],
        out_specs=(vmem, vmem),
        scratch_shapes=[
            pltpu.VMEM((WIDTH, WIDTH), jnp.float32),
            pltpu.VMEM((WIDTH, WIDTH), jnp.bfloat16),
            pltpu.VMEM((WIDTH, WIDTH), jnp.bfloat16),
            pltpu.VMEM((2, RANK, WIDTH), jnp.float32),
            pltpu.SMEM((2, ISLANDS), jnp.int32),
            tiles(4, TILES),
            tiles(4, PEERS),
            tiles(2, ISLANDS),
            tiles(ISLANDS, 1), tiles(ISLANDS, 3), tiles(ISLANDS, 1), tiles(ISLANDS, 2), tiles(ISLANDS, 1),
            tiles(TILES, 1), tiles(TILES, 3), tiles(TILES, 1), tiles(TILES, 2), tiles(TILES, 1),
            pltpu.VMEM((2, RANK, 128), jnp.float32),
            pltpu.VMEM((2, SIDE, RANK, 128), jnp.float32),
            dma((5,)), dma((4,)), dma((4,)), dma((5,)), dma((5,)), dma((2,)), dma((2,)),
            pltpu.SemaphoreType.REGULAR,
        ],
        compiler_params=pltpu.CompilerParams(
            collective_id=0, has_side_effects=True, vmem_limit_bytes=56 * 2**20
        ),
        name="exchange",
    )(weights, bases, pairs.transpose(0, 2, 1))
    rows = 256
    return pl.pallas_call(
        update_kernel,
        out_shape=jax.ShapeDtypeStruct(weights.shape, jnp.float32),
        grid=(WIDTH // rows,),
        in_specs=[pl.BlockSpec((1, rows, WIDTH), lambda i: (0, i, 0)), vmem, vmem],
        out_specs=pl.BlockSpec((1, rows, WIDTH), lambda i: (0, i, 0)),
        scratch_shapes=[pltpu.VMEM((6 * RANK, WIDTH), jnp.bfloat16)],
        name="update",
    )(weights, left, right)


def solution(mesh):
    in_specs = (P("island", "row", "col"), P(None, None, "col"), P())
    out_specs = P("island", "row", "col")
    return jax.shard_map(shards, mesh=mesh, in_specs=in_specs, out_specs=out_specs, check_vma=False)
```

time: 82.9 us -> 60.7 us (0.73); the launches traced: 81.7 us -> 60.5 us
  Pallas kernels: 76.4 us -> 60.5 us
  local copies, waits for them, and re-layouts: 5.28 us -> 0 us
    pallas_call x1, Pallas kernels: 70.8 us -> 55.1 us  [shards(): pl.pallas_call(exchange_kernel, out_shape=(factors, factors), in_specs=[a...]
    unnamed x9 -> x0, local copies, waits for them, and re-layouts: 5.28 us -> none
where the time goes in v2:
time: 60.7 us; the launch traced here: 60.5 us
  Pallas kernels  60.5 us (100%)
    pallas_call x1, Pallas kernels, shards(): pl.pallas_call(exchange_kernel, out_shape=(factors, factors), in_specs=[a...  55.1 us
    pallas_call x1, Pallas kernels, shards(): pl.pallas_call(update_kernel, out_shape=jax.ShapeDtypeStruct(weights.shap...  5.39 us

profile of v2, /device:TPU:1, one launch (start us, length us, event | category | flops | bytes accessed | tf_op | source)
XLA Modules:
  0.0 60.5 jit_solution(15386790435375886968)
XLA Ops:
  0.0 55.1 %exchange.1 = (f32[64,1024]{1,0:T(8,128)}, f32[64,1024]{1,0:T(8,128)}) custom-call(f32[1,1024,1024]{2,1,0:T(8,128)} %weights_ref.3, f32[2,32,1024]{2,1,0:T(8,128)} %bases_ref.1, s32[2,2,8]{2,1,0:T(2,128)} %bitcast.1), custom_call_target="tpu_custom_call" | custom-call | tf_op jit(solution)/shard_map/exchange/pallas_call | solution.py:426
  55.1 5.4 %update.1 = f32[1,1024,1024]{2,1,0:T(8,128)} custom-call(f32[1,1024,1024]{2,1,0:T(8,128)} %weights_ref.3, f32[64,1024]{1,0:T(8,128)} %get-tuple-element.7.left_ref, f32[64,1024]{1,0:T(8,128)} %get-tuple-element.8.right_ref), custom_call_target="tpu_custom_call" | custom-call | tf_op jit(solution)/shard_map/update/pallas_call | solution.py:453

commit v3 on v2

v3 whole, which is shorter than its diff:
```python
import jax
import jax.numpy as jnp
from jax import lax
from jax.experimental import pallas as pl
from jax.experimental.pallas import tpu as pltpu
from jax.sharding import PartitionSpec as P

MESH = pl.DeviceIdType.MESH
RANK = 32
WIDTH = 1024
TILES = 32
BLOCKS = WIDTH // 128
ISLANDS = 16
SIDE = 4
PEERS = ISLANDS * SIDE
HIGHEST = lax.Precision.HIGHEST
LAST = (((1,), (1,)), ((), ()))
FIRST = (((0,), (0,)), ((), ()))
PLAIN = (((1,), (0,)), ((), ()))


def halves(array):
    high = array.astype(jnp.bfloat16)
    low = (array - high.astype(jnp.float32)).astype(jnp.bfloat16)
    return high, low


def device(island, row, col):
    return {"island": island, "row": row, "col": col}


def exact_dot(left, right, dims):
    return lax.dot_general(left, right, dims, precision=HIGHEST, preferred_element_type=jnp.float32)


def fast_dot(left, right, dims):
    return lax.dot_general(left, right, dims, preferred_element_type=jnp.float32)


def stack(*rows):
    return jnp.concatenate(rows, axis=0)


def eliminate(matrix, double):
    rows = lax.broadcasted_iota(jnp.int32, (RANK, 128), 0)
    lanes = lax.broadcasted_iota(jnp.int32, (1, 128), 1)
    for pivot in range(RANK):
        factor = matrix[:, pivot : pivot + 1]
        here = lanes == pivot
        if double:
            factor = jnp.where(lanes < 64, factor, matrix[:, 64 + pivot : 65 + pivot])
            here = here | (lanes == 64 + pivot)
        else:
            factor = jnp.broadcast_to(factor, (RANK, 128))
        scaled = jnp.where(here, 1.0, matrix[pivot : pivot + 1]) / factor[pivot : pivot + 1]
        rest = jnp.where(here, 0.0, matrix) - factor * scaled
        matrix = jnp.where(rows == pivot, scaled, rest)
    return matrix


def exchange_kernel(
    weights_ref, bases_ref, pairs_ref, left_ref, right_ref, plain,
    high_ref, low_ref, bases_in, partner, first, arrived_first, sent, arrived, summed,
    pair_out, late_out, sums_out, last_out, pair_in, late_in, sums_in, last_in,
    factors_in, fold_sent, fold_got, gram_sent, gram_got,
    load_sem, send_sem, own_sem, back_sem, get_sem, mate_send, mate_sem, gram_send, gram_sem, ready_sem,
):
    island, row, col = (lax.axis_index(name) for name in ("island", "row", "col"))
    side, core = col // 2, col % 2
    other = (1 - side) * 2 + core
    mate = side * 2 + 1 - core

    barrier = pltpu.get_barrier_semaphore()

    def greet(index, carry):
        k, m = index // SIDE, index % SIDE

        @pl.when((k != island) | (m != col))
        def _():
            pl.semaphore_signal(barrier, inc=1, device_id=device(k, row, m), device_id_type=MESH)

        return carry

    lax.fori_loop(0, PEERS, greet, 0)
    for step in range(1, SIDE):
        pl.semaphore_signal(
            barrier, inc=1, device_id=device(island, (row + step) % SIDE, col), device_id_type=MESH
        )

    base_load = pltpu.make_async_copy(bases_ref, bases_in, load_sem.at[4])
    base_load.start()
    loads = []
    for part in range(4):
        rows = pl.ds(part * 256, 256)
        load = pltpu.make_async_copy(
            weights_ref.at[0, rows, :], plain.at[rows, :], load_sem.at[part]
        )
        load.start()
        loads.append(load)

    def find(index, carry):
        for matching in range(2):
            found = jnp.int32(0)
            for pair in range(ISLANDS // 2):
                first, second = pairs_ref[matching, 0, pair], pairs_ref[matching, 1, pair]
                found += jnp.where(first == index, second, 0) + jnp.where(second == index, first, 0)
            partner[matching, index] = found
        return carry

    lax.fori_loop(0, ISLANDS, find, 0)

    base_load.wait()
    base_high, base_low = halves(bases_in[...].reshape(2 * RANK, WIDTH))
    base_stack = stack(base_high, base_low)

    def put_first(value, part):
        for basis in range(2):
            for a in range(4):
                for b in range(2):
                    first[a * BLOCKS + part * 2 + b, basis] = value[
                        basis * RANK + a * 8 : basis * RANK + a * 8 + 8, b * 128 : b * 128 + 128
                    ]

    def put(flow, value, part):
        for a in range(4):
            for b in range(2):
                sent[flow, a * BLOCKS + part * 2 + b] = value[a * 8 : a * 8 + 8, b * 128 : b * 128 + 128]

    for part in range(4):
        loads[part].wait()
        rows = pl.ds(part * 256, 256)
        high, low = halves(plain[rows, :])
        high_ref[rows, :] = high
        low_ref[rows, :] = low
        wide = fast_dot(base_stack, high, LAST)
        fine = fast_dot(base_high, low, LAST)
        terms = wide[: 2 * RANK] + (wide[2 * RANK :] + fine)
        put_first(terms, part)

    pl.semaphore_wait(barrier, PEERS - 1 + SIDE - 1)
    for step in range(1, SIDE):
        pl.semaphore_signal(
            ready_sem, inc=1, device_id=device(island, (row + step) % SIDE, col), device_id_type=MESH
        )

    row_owner = core == island % 2
    row_tile = island * 2 + side
    col_owner = row % 2 == (island + core) % 2
    col_tile = island * 2 + row // 2

    def sized(ref, send, recv):
        return pltpu.make_async_remote_copy(
            ref, ref, send, recv, device_id=device(island, row, other), device_id_type=MESH
        )

    def add_up(flow):
        for k in range(ISLANDS):
            summed[flow, k] = (arrived[flow, k * 4] + arrived[flow, k * 4 + 1]) + (
                arrived[flow, k * 4 + 2] + arrived[flow, k * 4 + 3]
            )

    def send_over_columns():
        def send(index, carry):
            tile = (index + 2 * island) % TILES
            k = tile // 2
            m = (tile % 2) * 2 + k % 2

            @pl.when((k != island) | (m != col))
            def _():
                pltpu.make_async_remote_copy(
                    first.at[tile], arrived_first.at[island * 4 + col],
                    send_sem.at[0], own_sem.at[0],
                    device_id=device(k, row, m), device_id_type=MESH,
                ).start()

            return carry

        lax.fori_loop(0, TILES, send, 0)

    def give_pairs():
        def give(index, carry):
            k, m = (index // SIDE + island) % ISLANDS, index % SIDE

            @pl.when((k != island) | (m != col))
            def _():
                pltpu.make_async_remote_copy(
                    pair_out.at[m % 2, k], pair_in.at[row_tile], back_sem.at[0], get_sem.at[0],
                    device_id=device(k, row, m), device_id_type=MESH,
                ).start()

            return carry

        lax.fori_loop(0, PEERS, give, 0)
        pair_in[row_tile] = pair_out[core, island]

    def give_late():
        def give(index, carry):
            k = (index // 2 + island) % ISLANDS
            m = (index % 2) * 2 + row_tile // 16

            @pl.when((k != island) | (m != col))
            def _():
                pltpu.make_async_remote_copy(
                    late_out.at[k], late_in.at[row_tile], back_sem.at[1], get_sem.at[1],
                    device_id=device(k, row, m), device_id_type=MESH,
                ).start()

            return carry

        lax.fori_loop(0, 2 * ISLANDS, give, 0)

        @pl.when(row_tile // 16 == core)
        def _():
            late_in[row_tile] = late_out[island]

    def send_over_rows(flow):
        def send(index, carry):
            tile = (index + 2 * island) % TILES
            k = tile // 2
            m = (tile % 2) * 2 + (k + core) % 2
            pltpu.make_async_remote_copy(
                sent.at[flow, tile], arrived.at[flow, island * 4 + row],
                send_sem.at[flow + 1], own_sem.at[flow + 1],
                device_id=device(k, m, other), device_id_type=MESH,
            ).start()
            return carry

        lax.fori_loop(0, TILES, send, 0)

    def owned_over_rows(flow):
        sized(arrived.at[flow], send_sem.at[flow + 1], own_sem.at[flow + 1]).wait_recv()
        add_up(flow)

    def give_over_rows(flow, out, into):
        def give(index, carry):
            k, m = (index // SIDE + island) % ISLANDS, index % SIDE
            pltpu.make_async_remote_copy(
                out.at[k], into.at[col_tile], back_sem.at[flow], get_sem.at[flow],
                device_id=device(k, m, other), device_id_type=MESH,
            ).start()
            return carry

        lax.fori_loop(0, PEERS, give, 0)

    def whole(ref, which):
        return stack(
            *(
                jnp.concatenate([ref[a * BLOCKS + b, which] for b in range(BLOCKS)], axis=1)
                for a in range(4)
            )
        )

    def to_mate(source, target, index):
        copy = pltpu.make_async_remote_copy(
            source, target, mate_send.at[index], mate_sem.at[index],
            device_id=device(island, row, mate), device_id_type=MESH,
        )
        copy.start()
        return copy

    def gram_start(gram):
        gram_sent[...] = gram
        gram_got[row] = gram
        for step in range(1, SIDE):
            pltpu.make_async_remote_copy(
                gram_sent, gram_got.at[row], gram_send.at[1], gram_sem.at[1],
                device_id=device(island, (row + step) % SIDE, col), device_id_type=MESH,
            ).start()

    def gram_finish():
        sized(gram_got.at[pl.ds(0, SIDE - 1)], gram_send.at[1], gram_sem.at[1]).wait_recv()
        return (gram_got[0] + gram_got[1]) + (gram_got[2] + gram_got[3])

    def times_weights(high, low, count, use):
        both = stack(high, low)
        for part in range(4):
            cols = pl.ds(part * 256, 256)
            wide = fast_dot(both, high_ref[:, cols], PLAIN)
            fine = fast_dot(high, low_ref[:, cols], PLAIN)
            use(wide[:count] + (wide[count:] + fine), part)

    send_over_columns()

    @pl.when(row_owner)
    def _():
        arrived_first[island * 4 + col] = first[row_tile]
        sized(arrived_first.at[pl.ds(0, PEERS - 1)], send_sem.at[0], own_sem.at[0]).wait_recv()
        for k in range(ISLANDS):
            for basis in range(2):
                summed[basis, k] = (
                    arrived_first[k * 4, basis] + arrived_first[k * 4 + 1, basis]
                ) + (arrived_first[k * 4 + 2, basis] + arrived_first[k * 4 + 3, basis])
        for k in range(ISLANDS):
            for basis in range(2):
                pair_out[0, k, basis] = summed[basis, k] - summed[basis, partner[0, k]]
        for k in range(ISLANDS):
            pair_out[1, k] = pair_out[0, partner[1, k]]
        give_pairs()
        for k in range(ISLANDS):
            late_out[k, 0] = summed[1, k] - summed[1, partner[1, k]]
        give_late()
        sized(pair_in.at[pl.ds(0, TILES - 1)], back_sem.at[0], get_sem.at[0]).wait_recv()

    @pl.when(jnp.logical_not(row_owner))
    def _():
        sized(pair_in, back_sem.at[0], get_sem.at[0]).wait_recv()

    mine = whole(pair_in, 0)
    factors_in[core] = mine
    mate_copies = [to_mate(factors_in.at[core], factors_in.at[core], 0)]
    mine_high, mine_low = halves(mine)
    cross_high, cross_low = halves(whole(pair_in, 1))
    block = fast_dot(
        stack(mine_high, mine_low),
        stack(mine_high, cross_high, mine_high, cross_high, mine_low, cross_low, mine_low, cross_low),
        LAST,
    )
    block = block[:RANK, :128] + (block[:RANK, 128:] + block[RANK:, :128])
    narrow = lax.broadcasted_iota(jnp.int32, (RANK // 2, 128), 1) < 64
    fold_sent[...] = jnp.where(narrow, block[: RANK // 2], block[RANK // 2 :])
    fold_got[core, row] = fold_sent[...]

    def fold(index, carry):
        m, h = (row + 1 + index // 2) % SIDE, index % 2

        @pl.when((m != row) | (h != core))
        def _():
            pltpu.make_async_remote_copy(
                fold_sent, fold_got.at[core, row], gram_send.at[0], gram_sem.at[0],
                device_id=device(island, m, side * 2 + h), device_id_type=MESH,
            ).start()

        return carry

    lax.fori_loop(0, 2 * SIDE, fold, 0)

    late_share = row_owner & (row_tile // 16 == core)

    @pl.when(late_share)
    def _():
        sized(late_in.at[pl.ds(0, TILES // 2 - 1)], back_sem.at[1], get_sem.at[1]).wait_recv()

    @pl.when(jnp.logical_not(late_share))
    def _():
        sized(late_in.at[pl.ds(0, TILES // 2)], back_sem.at[1], get_sem.at[1]).wait_recv()

    share = late_in.at[pl.ds(core * 16, 16)]
    mate_copies.append(to_mate(share, share, 1))
    for copy in mate_copies:
        copy.wait_recv()
    near, far, late = factors_in[0], factors_in[1], whole(late_in, 0)
    near_high, near_low = halves(near)
    far_high, far_low = halves(far)
    late_high, late_low = halves(late)
    products = []

    def use(value, part):
        put(0, value[:RANK], part)
        products.append(value)

    times_weights(stack(near_high, late_high, far_high), stack(near_low, late_low, far_low), 3 * RANK, use)
    pl.semaphore_wait(ready_sem, SIDE - 1)
    send_over_rows(0)
    products = jnp.concatenate(products, axis=1)
    later = products[RANK:]
    near_product = products[:RANK]
    product_high, product_low = halves(stack(near_product, later[RANK:]))

    sized(arrived_first.at[pl.ds(0, 2 * SIDE - 1)], gram_send.at[0], gram_sem.at[0]).wait_recv()
    near_fold, far_fold = (
        (fold_got[h, 0] + fold_got[h, 1]) + (fold_got[h, 2] + fold_got[h, 3]) for h in range(2)
    )
    solved = eliminate(
        stack(
            jnp.where(narrow, near_fold, pltpu.roll(far_fold, 64, 1)),
            jnp.where(narrow, pltpu.roll(near_fold, 64, 1), far_fold),
        ),
        True,
    )
    near_inverse, far_inverse = solved[:, :32], solved[:, 64:96]
    mixing = 0.5 * stack(-solved[:, 32:64], solved[:, 96:128])
    mixing_high, mixing_low = halves(mixing)

    def mixed(high, low):
        return fast_dot(mixing_high, high, FIRST) + (
            fast_dot(mixing_high, low, FIRST) + fast_dot(mixing_low, high, FIRST)
        )

    terms = later[:RANK] + mixed(product_high, product_low)
    for part in range(4):
        put(1, terms[:, part * 256 : part * 256 + 256], part)
    send_over_rows(1)

    factor = late + mixed(stack(near_high, far_high), stack(near_low, far_low))
    factor_high, factor_low = halves(factor)
    nothing = jnp.zeros((RANK, WIDTH), jnp.bfloat16)
    block = fast_dot(
        stack(factor_high, factor_low),
        stack(
            factor_high, near_high, far_high, nothing,
            factor_low, near_low, far_low, nothing,
        ),
        LAST,
    )
    gram_start(block[:RANK, :128] + (block[:RANK, 128:] + block[RANK:, :128]))

    @pl.when(col_owner)
    def _():
        owned_over_rows(0)
        for k in range(ISLANDS):
            sums_out[k, 0] = summed[0, k] + summed[0, partner[0, k]]
        for k in range(ISLANDS):
            sums_out[k, 1] = sums_out[partner[1, k], 0]
        give_over_rows(2, sums_out, sums_in)

    left_ref[:RANK, :] = 0.5 * exact_dot(near_inverse, near, PLAIN)

    @pl.when(col_owner)
    def _():
        owned_over_rows(1)
        for k in range(ISLANDS):
            last_out[k, 0] = summed[1, k] + summed[1, partner[1, k]]
        give_over_rows(3, last_out, last_in)

    crossed = gram_finish()
    left_ref[RANK:, :] = 0.5 * exact_dot(eliminate(crossed, False)[:, :32], factor, PLAIN)
    near_change = -0.5 * exact_dot(crossed[:, 32:64], near_inverse, PLAIN)
    far_change = 0.5 * exact_dot(crossed[:, 64:96], far_inverse, PLAIN)
    sized(sums_in, back_sem.at[2], get_sem.at[2]).wait_recv()
    near_sums = whole(sums_in, 0)
    right_ref[:RANK, :] = near_sums
    change = exact_dot(
        jnp.concatenate([near_change, far_change], axis=1), stack(near_sums, whole(sums_in, 1)), PLAIN
    )
    sized(last_in, back_sem.at[3], get_sem.at[3]).wait_recv()
    right_ref[RANK:, :] = whole(last_in, 0) + change

    for copy in mate_copies:
        copy.wait_send()
    sized(arrived_first.at[pl.ds(0, 2 * SIDE - 1)], gram_send.at[0], gram_sem.at[0]).wait_send()
    sized(gram_got.at[pl.ds(0, SIDE - 1)], gram_send.at[1], gram_sem.at[1]).wait_send()
    for flow in range(2):
        sized(sent.at[flow], send_sem.at[flow + 1], own_sem.at[flow + 1]).wait_send()

    @pl.when(row_owner)
    def _():
        sized(first.at[pl.ds(0, TILES - 1)], send_sem.at[0], own_sem.at[0]).wait_send()
        sized(arrived_first.at[pl.ds(0, PEERS - 1)], back_sem.at[0], get_sem.at[0]).wait_send()

        @pl.when(late_share)
        def _():
            sized(late_in.at[pl.ds(0, 2 * ISLANDS - 1)], back_sem.at[1], get_sem.at[1]).wait_send()

        @pl.when(jnp.logical_not(late_share))
        def _():
            sized(late_in, back_sem.at[1], get_sem.at[1]).wait_send()

    @pl.when(jnp.logical_not(row_owner))
    def _():
        sized(first, send_sem.at[0], own_sem.at[0]).wait_send()

    @pl.when(col_owner)
    def _():
        for flow, count in ((2, 2), (3, 1)):
            sized(arrived.at[pl.ds(0, count)], back_sem.at[flow], get_sem.at[flow]).wait_send()


def update_kernel(weights_ref, left_ref, right_ref, out_ref, updated, sem):
    parts, rows = updated.shape[:2]
    high, low = halves(right_ref[...])
    right_stack = stack(high, low, high)
    copies = []
    for part in range(parts):
        block = pl.ds(part * rows, rows)
        high, low = halves(left_ref[:, block])
        updated[part] = weights_ref[block, :] - fast_dot(stack(high, high, low), right_stack, FIRST)
        copy = pltpu.make_async_copy(updated.at[part], out_ref.at[0, block, :], sem.at[part])
        copy.start()
        copies.append(copy)
    for copy in copies:
        copy.wait()


def shards(weights, bases, pairs):
    vmem = pl.BlockSpec(memory_space=pltpu.VMEM)
    hbm = pl.BlockSpec(memory_space=pltpu.HBM)
    factors = jax.ShapeDtypeStruct((2 * RANK, WIDTH), jnp.float32)
    tile = jax.ShapeDtypeStruct((WIDTH, WIDTH), jnp.float32)

    def tiles(*lead):
        return pltpu.VMEM((*lead, 8, 128), jnp.float32)

    dma = pltpu.SemaphoreType.DMA
    left, right, plain = pl.pallas_call(
        exchange_kernel,
        out_shape=(factors, factors, tile),
        in_specs=[hbm, hbm, pl.BlockSpec(memory_space=pltpu.SMEM)],
        out_specs=(vmem, vmem, vmem),
        scratch_shapes=[
            pltpu.VMEM((WIDTH, WIDTH), jnp.bfloat16),
            pltpu.VMEM((WIDTH, WIDTH), jnp.bfloat16),
            pltpu.VMEM((2, RANK, WIDTH), jnp.float32),
            pltpu.SMEM((2, ISLANDS), jnp.int32),
            tiles(TILES, 2), tiles(PEERS, 2),
            tiles(2, TILES), tiles(2, PEERS), tiles(2, ISLANDS),
            tiles(2, ISLANDS, 2), tiles(ISLANDS, 1), tiles(ISLANDS, 2), tiles(ISLANDS, 1),
            tiles(TILES, 2), tiles(TILES, 1), tiles(TILES, 2), tiles(TILES, 1),
            pltpu.VMEM((2, RANK, WIDTH), jnp.float32),
            pltpu.VMEM((RANK // 2, 128), jnp.float32),
            pltpu.VMEM((2, SIDE, RANK // 2, 128), jnp.float32),
            pltpu.VMEM((RANK, 128), jnp.float32),
            pltpu.VMEM((SIDE, RANK, 128), jnp.float32),
            dma((5,)), dma((3,)), dma((3,)), dma((4,)), dma((4,)), dma((2,)), dma((2,)), dma((2,)), dma((2,)),
            pltpu.SemaphoreType.REGULAR,
        ],
        compiler_params=pltpu.CompilerParams(
            collective_id=0, has_side_effects=True, vmem_limit_bytes=32 * 2**20
        ),
        name="exchange",
    )(*(pltpu.with_memory_space_constraint(x, pltpu.HBM) for x in (weights, bases, pairs.transpose(0, 2, 1))))
    parts = 8
    return pl.pallas_call(
        update_kernel,
        out_shape=jax.ShapeDtypeStruct(weights.shape, jnp.float32),
        in_specs=[vmem, vmem, vmem],
        out_specs=hbm,
        scratch_shapes=[pltpu.VMEM((parts, WIDTH // parts, WIDTH), jnp.float32), dma((parts,))],
        compiler_params=pltpu.CompilerParams(vmem_limit_bytes=20 * 2**20),
        name="update",
    )(plain, left, right)


def solution(mesh):
    in_specs = (P("island", "row", "col"), P(None, None, "col"), P())
    out_specs = P("island", "row", "col")
    return jax.shard_map(shards, mesh=mesh, in_specs=in_specs, out_specs=out_specs, check_vma=False)
```

time: 60.7 us -> 55.2 us (0.909)
  Pallas kernels: 60.5 us -> 55.1 us
    pallas_call x1, Pallas kernels: 5.39 us -> 2.33 us  [shards(): pl.pallas_call(update_kernel, out_shape=jax.ShapeDtypeStruct(weights.shap...]
    pallas_call x1, Pallas kernels: 55.1 us -> 52.7 us  [shards(): pl.pallas_call(exchange_kernel, out_shape=(factors, factors, tile), in_sp...]
where the time goes in v3:
time: 55.2 us; the launch traced here: 55.1 us
  Pallas kernels  55.1 us (100%)
    pallas_call x1, Pallas kernels, shards(): pl.pallas_call(exchange_kernel, out_shape=(factors, factors, tile), in_sp...  52.7 us
    pallas_call x1, Pallas kernels, shards(): pl.pallas_call(update_kernel, out_shape=jax.ShapeDtypeStruct(weights.shap...  2.33 us

profile of v3, /device:TPU:1, one launch (start us, length us, event | category | flops | bytes accessed | tf_op | source)
XLA Modules:
  0.0 55.1 jit_solution(11630247073017822251)
XLA Ops:
  0.0 52.7 %exchange.1 = (f32[64,1024]{1,0:T(8,128)S(1)}, f32[64,1024]{1,0:T(8,128)S(1)}, f32[1024,1024]{1,0:T(8,128)S(1)}) custom-call(f32[1,1024,1024]{2,1,0:T(8,128)} %weights_ref.1, f32[2,32,1024]{2,1,0:T(8,128)} %bases_ref.1, s32[2,2,8]{2,1,0:T(2,128)} %bitcast.1), custom_call_target="tpu_custom_call" | custom-call | tf_op jit(solution)/shard_map/exchange/pallas_call | solution.py:494
  52.8 2.3 %update.1 = f32[1,1024,1024]{2,1,0:T(8,128)} custom-call(f32[1024,1024]{1,0:T(8,128)S(1)} %get-tuple-element.8.weights_ref, f32[64,1024]{1,0:T(8,128)S(1)} %get-tuple-element.9.left_ref, f32[64,1024]{1,0:T(8,128)S(1)} %get-tuple-element.10.right_ref), custom_call_target="tpu_custom_call" | custom-call | tf_op jit(solution)/shard_map/update/pallas_call | solution.py:522

commit v4 on v3

--- a/solution.py
+++ b/solution.py
@@ -13,6 +13,7 @@
 ISLANDS = 16
 SIDE = 4
 PEERS = ISLANDS * SIDE
+BLOCK = 4
 HIGHEST = lax.Precision.HIGHEST
 LAST = (((1,), (1,)), ((), ()))
 FIRST = (((0,), (0,)), ((), ()))
@@ -44,17 +45,41 @@
 def eliminate(matrix, double):
     rows = lax.broadcasted_iota(jnp.int32, (RANK, 128), 0)
     lanes = lax.broadcasted_iota(jnp.int32, (1, 128), 1)
-    for pivot in range(RANK):
-        factor = matrix[:, pivot : pivot + 1]
-        here = lanes == pivot
-        if double:
-            factor = jnp.where(lanes < 64, factor, matrix[:, 64 + pivot : 65 + pivot])
-            here = here | (lanes == 64 + pivot)
-        else:
-            factor = jnp.broadcast_to(factor, (RANK, 128))
-        scaled = jnp.where(here, 1.0, matrix[pivot : pivot + 1]) / factor[pivot : pivot + 1]
-        rest = jnp.where(here, 0.0, matrix) - factor * scaled
-        matrix = jnp.where(rows == pivot, scaled, rest)
+    position = lanes % 64 if double else lanes
+    for start in range(0, RANK, BLOCK):
+        pivots = range(start, start + BLOCK)
+        factors = []
+        for pivot in pivots:
+            factor = jnp.broadcast_to(matrix[:, pivot : pivot + 1], (RANK, 128))
+            if double:
+                second = jnp.broadcast_to(matrix[:, 64 + pivot : 65 + pivot], (RANK, 128))
+                factor = jnp.where(lanes < 64, factor, second)
+            factors.append(factor)
+        here = (position >= start) & (position < start + BLOCK)
+        solved = [
+            jnp.where(here, jnp.where(position == pivot, 1.0, 0.0), matrix[pivot : pivot + 1])
+            for pivot in pivots
+        ]
+        corner = [[factor[pivot : pivot + 1] for factor in factors] for pivot in pivots]
+        for j in range(BLOCK):
+            scale = 1.0 / corner[j][j]
+            solved[j] = solved[j] * scale
+            corner[j] = [entry * scale if m > j else entry for m, entry in enumerate(corner[j])]
+            for i in range(j + 1, BLOCK):
+                solved[i] = solved[i] - corner[i][j] * solved[j]
+                corner[i] = [
+                    entry - corner[i][j] * corner[j][m] if m > j else entry
+                    for m, entry in enumerate(corner[i])
+                ]
+        for j in reversed(range(BLOCK)):
+            for i in range(j):
+                solved[i] = solved[i] - corner[i][j] * solved[j]
+        rest = jnp.where(here, 0.0, matrix)
+        for factor, row in zip(factors, solved):
+            rest = rest - factor * row
+        for pivot, row in zip(pivots, solved):
+            rest = jnp.where(rows == pivot, row, rest)
+        matrix = rest
     return matrix
 
 
@@ -70,23 +95,6 @@
     other = (1 - side) * 2 + core
     mate = side * 2 + 1 - core
 
-    barrier = pltpu.get_barrier_semaphore()
-
-    def greet(index, carry):
-        k, m = index // SIDE, index % SIDE
-
-        @pl.when((k != island) | (m != col))
-        def _():
-            pl.semaphore_signal(barrier, inc=1, device_id=device(k, row, m), device_id_type=MESH)
-
-        return carry
-
-    lax.fori_loop(0, PEERS, greet, 0)
-    for step in range(1, SIDE):
-        pl.semaphore_signal(
-            barrier, inc=1, device_id=device(island, (row + step) % SIDE, col), device_id_type=MESH
-        )
-
     base_load = pltpu.make_async_copy(bases_ref, bases_in, load_sem.at[4])
     base_load.start()
     loads = []
@@ -98,16 +106,30 @@
         load.start()
         loads.append(load)
 
-    def find(index, carry):
-        for matching in range(2):
-            found = jnp.int32(0)
-            for pair in range(ISLANDS // 2):
-                first, second = pairs_ref[matching, 0, pair], pairs_ref[matching, 1, pair]
-                found += jnp.where(first == index, second, 0) + jnp.where(second == index, first, 0)
-            partner[matching, index] = found
+    barrier = pltpu.get_barrier_semaphore()
+    across, along = island // SIDE, island % SIDE
+
+    def far_first(index):
+        return (2 + 3 * index + 3 * (index * (index - 1) // 2)) % SIDE
+
+    def far_island(index):
+        return (across + far_first(index // SIDE)) % SIDE * SIDE + (along + far_first(index % SIDE)) % SIDE
+
+    def greet(index, carry):
+        k = far_island(index)
+        for m in range(SIDE):
+
+            @pl.when((k != island) | (m != col))
+            def _():
+                pl.semaphore_signal(barrier, inc=1, device_id=device(k, row, m), device_id_type=MESH)
+
         return carry
 
-    lax.fori_loop(0, ISLANDS, find, 0)
+    lax.fori_loop(0, ISLANDS, greet, 0)
+    for step in range(1, SIDE):
+        pl.semaphore_signal(
+            barrier, inc=1, device_id=device(island, (row + step) % SIDE, col), device_id_type=MESH
+        )
 
     base_load.wait()
     base_high, base_low = halves(bases_in[...].reshape(2 * RANK, WIDTH))
@@ -161,53 +183,55 @@
 
     def send_over_columns():
         def send(index, carry):
-            tile = (index + 2 * island) % TILES
-            k = tile // 2
-            m = (tile % 2) * 2 + k % 2
-
-            @pl.when((k != island) | (m != col))
-            def _():
-                pltpu.make_async_remote_copy(
-                    first.at[tile], arrived_first.at[island * 4 + col],
-                    send_sem.at[0], own_sem.at[0],
-                    device_id=device(k, row, m), device_id_type=MESH,
-                ).start()
+            k = far_island(index)
+            for which in range(2):
+                m = which * 2 + k % 2
+
+                @pl.when((k != island) | (m != col))
+                def _():
+                    pltpu.make_async_remote_copy(
+                        first.at[2 * k + which], arrived_first.at[island * 4 + col],
+                        send_sem.at[0], own_sem.at[0],
+                        device_id=device(k, row, m), device_id_type=MESH,
+                    ).start()
 
             return carry
 
-        lax.fori_loop(0, TILES, send, 0)
+        lax.fori_loop(0, ISLANDS, send, 0)
 
     def give_pairs():
         def give(index, carry):
-            k, m = (index // SIDE + island) % ISLANDS, index % SIDE
-
-            @pl.when((k != island) | (m != col))
-            def _():
-                pltpu.make_async_remote_copy(
-                    pair_out.at[m % 2, k], pair_in.at[row_tile], back_sem.at[0], get_sem.at[0],
-                    device_id=device(k, row, m), device_id_type=MESH,
-                ).start()
+            k = far_island(index)
+            for m in range(SIDE):
+
+                @pl.when((k != island) | (m != col))
+                def _():
+                    pltpu.make_async_remote_copy(
+                        pair_out.at[m % 2, k], pair_in.at[row_tile], back_sem.at[0], get_sem.at[0],
+                        device_id=device(k, row, m), device_id_type=MESH,
+                    ).start()
 
             return carry
 
-        lax.fori_loop(0, PEERS, give, 0)
+        lax.fori_loop(0, ISLANDS, give, 0)
         pair_in[row_tile] = pair_out[core, island]
 
     def give_late():
         def give(index, carry):
-            k = (index // 2 + island) % ISLANDS
-            m = (index % 2) * 2 + row_tile // 16
-
-            @pl.when((k != island) | (m != col))
-            def _():
-                pltpu.make_async_remote_copy(
-                    late_out.at[k], late_in.at[row_tile], back_sem.at[1], get_sem.at[1],
-                    device_id=device(k, row, m), device_id_type=MESH,
-                ).start()
+            k = far_island(index)
+            for half in range(2):
+                m = half * 2 + row_tile // 16
+
+                @pl.when((k != island) | (m != col))
+                def _():
+                    pltpu.make_async_remote_copy(
+                        late_out.at[k], late_in.at[row_tile], back_sem.at[1], get_sem.at[1],
+                        device_id=device(k, row, m), device_id_type=MESH,
+                    ).start()
 
             return carry
 
-        lax.fori_loop(0, 2 * ISLANDS, give, 0)
+        lax.fori_loop(0, ISLANDS, give, 0)
 
         @pl.when(row_tile // 16 == core)
         def _():
@@ -215,17 +239,16 @@
 
     def send_over_rows(flow):
         def send(index, carry):
-            tile = (index + 2 * island) % TILES
-            k = tile // 2
-            m = (tile % 2) * 2 + (k + core) % 2
-            pltpu.make_async_remote_copy(
-                sent.at[flow, tile], arrived.at[flow, island * 4 + row],
-                send_sem.at[flow + 1], own_sem.at[flow + 1],
-                device_id=device(k, m, other), device_id_type=MESH,
-            ).start()
+            k = far_island(index)
+            for which in range(2):
+                pltpu.make_async_remote_copy(
+                    sent.at[flow, 2 * k + which], arrived.at[flow, island * 4 + row],
+                    send_sem.at[flow + 1], own_sem.at[flow + 1],
+                    device_id=device(k, which * 2 + (k + core) % 2, other), device_id_type=MESH,
+                ).start()
             return carry
 
-        lax.fori_loop(0, TILES, send, 0)
+        lax.fori_loop(0, ISLANDS, send, 0)
 
     def owned_over_rows(flow):
         sized(arrived.at[flow], send_sem.at[flow + 1], own_sem.at[flow + 1]).wait_recv()
@@ -233,14 +256,16 @@
 
     def give_over_rows(flow, out, into):
         def give(index, carry):
-            k, m = (index // SIDE + island) % ISLANDS, index % SIDE
-            pltpu.make_async_remote_copy(
-                out.at[k], into.at[col_tile], back_sem.at[flow], get_sem.at[flow],
-                device_id=device(k, m, other), device_id_type=MESH,
-            ).start()
+            k = far_island(index % ISLANDS)
+            for near in range(2):
+                m = (row + 1 + side + near + 2 * (index // ISLANDS)) % SIDE
+                pltpu.make_async_remote_copy(
+                    out.at[k], into.at[col_tile], back_sem.at[flow], get_sem.at[flow],
+                    device_id=device(k, m, other), device_id_type=MESH,
+                ).start()
             return carry
 
-        lax.fori_loop(0, PEERS, give, 0)
+        lax.fori_loop(0, 2 * ISLANDS, give, 0)
 
     def whole(ref, which):
         return stack(
@@ -280,6 +305,17 @@
             use(wide[:count] + (wide[count:] + fine), part)
 
     send_over_columns()
+
+    def find(index, carry):
+        for matching in range(2):
+            found = jnp.int32(0)
+            for pair in range(ISLANDS // 2):
+                first, second = pairs_ref[matching, 0, pair], pairs_ref[matching, 1, pair]
+                found += jnp.where(first == index, second, 0) + jnp.where(second == index, first, 0)
+            partner[matching, index] = found
+        return carry
+
+    lax.fori_loop(0, ISLANDS, find, 0)
 
     @pl.when(row_owner)
     def _():

time: 55.2 us -> 51.9 us (0.940)
  Pallas kernels: 55.1 us -> 51.8 us
    pallas_call x1, Pallas kernels: 52.7 us -> 49.4 us  [shards(): pl.pallas_call(exchange_kernel, out_shape=(factors, factors, tile), in_sp...]
where the time goes in v4:
time: 51.9 us; the launch traced here: 51.8 us
  Pallas kernels  51.8 us (100%)
    pallas_call x1, Pallas kernels, shards(): pl.pallas_call(exchange_kernel, out_shape=(factors, factors, tile), in_sp...  49.4 us
    pallas_call x1, Pallas kernels, shards(): pl.pallas_call(update_kernel, out_shape=jax.ShapeDtypeStruct(weights.shap...  2.35 us

profile of v4, /device:TPU:1, one launch (start us, length us, event | category | flops | bytes accessed | tf_op | source)
XLA Modules:
  0.0 51.8 jit_solution(8342495888274840764)
XLA Ops:
  0.0 49.4 %exchange.1 = (f32[64,1024]{1,0:T(8,128)S(1)}, f32[64,1024]{1,0:T(8,128)S(1)}, f32[1024,1024]{1,0:T(8,128)S(1)}) custom-call(f32[1,1024,1024]{2,1,0:T(8,128)} %weights_ref.1, f32[2,32,1024]{2,1,0:T(8,128)} %bases_ref.1, s32[2,2,8]{2,1,0:T(2,128)} %bitcast.1), custom_call_target="tpu_custom_call" | custom-call | tf_op jit(solution)/shard_map/exchange/pallas_call | solution.py:530
  49.5 2.4 %update.1 = f32[1,1024,1024]{2,1,0:T(8,128)} custom-call(f32[1024,1024]{1,0:T(8,128)S(1)} %get-tuple-element.8.weights_ref, f32[64,1024]{1,0:T(8,128)S(1)} %get-tuple-element.9.left_ref, f32[64,1024]{1,0:T(8,128)S(1)} %get-tuple-element.10.right_ref), custom_call_target="tpu_custom_call" | custom-call | tf_op jit(solution)/shard_map/update/pallas_call | solution.py:558

commit v5 on v4

--- a/solution.py
+++ b/solution.py
@@ -125,7 +125,7 @@
 
         return carry
 
-    lax.fori_loop(0, ISLANDS, greet, 0)
+    lax.fori_loop(0, ISLANDS, greet, 0, unroll=True)
     for step in range(1, SIDE):
         pl.semaphore_signal(
             barrier, inc=1, device_id=device(island, (row + step) % SIDE, col), device_id_type=MESH
@@ -197,7 +197,7 @@
 
             return carry
 
-        lax.fori_loop(0, ISLANDS, send, 0)
+        lax.fori_loop(0, ISLANDS, send, 0, unroll=True)
 
     def give_pairs():
         def give(index, carry):
@@ -213,7 +213,7 @@
 
             return carry
 
-        lax.fori_loop(0, ISLANDS, give, 0)
+        lax.fori_loop(0, ISLANDS, give, 0, unroll=True)
         pair_in[row_tile] = pair_out[core, island]
 
     def give_late():
@@ -231,7 +231,7 @@
 
             return carry
 
-        lax.fori_loop(0, ISLANDS, give, 0)
+        lax.fori_loop(0, ISLANDS, give, 0, unroll=True)
 
         @pl.when(row_tile // 16 == core)
         def _():
@@ -248,7 +248,7 @@
                 ).start()
             return carry
 
-        lax.fori_loop(0, ISLANDS, send, 0)
+        lax.fori_loop(0, ISLANDS, send, 0, unroll=True)
 
     def owned_over_rows(flow):
         sized(arrived.at[flow], send_sem.at[flow + 1], own_sem.at[flow + 1]).wait_recv()
@@ -265,7 +265,7 @@
                 ).start()
             return carry
 
-        lax.fori_loop(0, 2 * ISLANDS, give, 0)
+        lax.fori_loop(0, 2 * ISLANDS, give, 0, unroll=True)
 
     def whole(ref, which):
         return stack(
@@ -382,24 +382,28 @@
 
     share = late_in.at[pl.ds(core * 16, 16)]
     mate_copies.append(to_mate(share, share, 1))
-    for copy in mate_copies:
-        copy.wait_recv()
-    near, far, late = factors_in[0], factors_in[1], whole(late_in, 0)
+    mate_copies[0].wait_recv()
+    near, far = factors_in[0], factors_in[1]
     near_high, near_low = halves(near)
     far_high, far_low = halves(far)
-    late_high, late_low = halves(late)
-    products = []
-
-    def use(value, part):
-        put(0, value[:RANK], part)
-        products.append(value)
-
-    times_weights(stack(near_high, late_high, far_high), stack(near_low, late_low, far_low), 3 * RANK, use)
+    near_product, later = [], []
+
+    def use_near(value, part):
+        put(0, value, part)
+        near_product.append(value)
+
+    times_weights(near_high, near_low, RANK, use_near)
     pl.semaphore_wait(ready_sem, SIDE - 1)
     send_over_rows(0)
-    products = jnp.concatenate(products, axis=1)
-    later = products[RANK:]
-    near_product = products[:RANK]
+    mate_copies[1].wait_recv()
+    late = whole(late_in, 0)
+    late_high, late_low = halves(late)
+    times_weights(
+        stack(late_high, far_high), stack(late_low, far_low), 2 * RANK,
+        lambda value, part: later.append(value),
+    )
+    near_product = jnp.concatenate(near_product, axis=1)
+    later = jnp.concatenate(later, axis=1)
     product_high, product_low = halves(stack(near_product, later[RANK:]))
 
     sized(arrived_first.at[pl.ds(0, 2 * SIDE - 1)], gram_send.at[0], gram_sem.at[0]).wait_recv()

time: 51.9 us -> 51 us (0.983)
  Pallas kernels: 51.8 us -> 50.9 us
    pallas_call x1, Pallas kernels: 49.4 us -> 48.5 us  [shards(): pl.pallas_call(exchange_kernel, out_shape=(factors, factors, tile), in_sp...]
where the time goes in v5:
time: 51 us; the launch traced here: 50.9 us
  Pallas kernels  50.9 us (100%)
    pallas_call x1, Pallas kernels, shards(): pl.pallas_call(exchange_kernel, out_shape=(factors, factors, tile), in_sp...  48.5 us
    pallas_call x1, Pallas kernels, shards(): pl.pallas_call(update_kernel, out_shape=jax.ShapeDtypeStruct(weights.shap...  2.33 us

profile of v5, /device:TPU:1, one launch (start us, length us, event | category | flops | bytes accessed | tf_op | source)
XLA Modules:
  0.0 50.9 jit_solution(13754170255602599779)
XLA Ops:
  0.0 48.5 %exchange.1 = (f32[64,1024]{1,0:T(8,128)S(1)}, f32[64,1024]{1,0:T(8,128)S(1)}, f32[1024,1024]{1,0:T(8,128)S(1)}) custom-call(f32[1,1024,1024]{2,1,0:T(8,128)} %weights_ref.1, f32[2,32,1024]{2,1,0:T(8,128)} %bases_ref.1, s32[2,2,8]{2,1,0:T(2,128)} %bitcast.1), custom_call_target="tpu_custom_call" | custom-call | tf_op jit(solution)/shard_map/exchange/pallas_call | solution.py:534
  48.5 2.3 %update.1 = f32[1,1024,1024]{2,1,0:T(8,128)} custom-call(f32[1024,1024]{1,0:T(8,128)S(1)} %get-tuple-element.8.weights_ref, f32[64,1024]{1,0:T(8,128)S(1)} %get-tuple-element.9.left_ref, f32[64,1024]{1,0:T(8,128)S(1)} %get-tuple-element.10.right_ref), custom_call_target="tpu_custom_call" | custom-call | tf_op jit(solution)/shard_map/update/pallas_call | solution.py:562

commit v6 on v5

--- a/solution.py
+++ b/solution.py
@@ -88,7 +88,7 @@
     high_ref, low_ref, bases_in, partner, first, arrived_first, sent, arrived, summed,
     pair_out, late_out, sums_out, last_out, pair_in, late_in, sums_in, last_in,
     factors_in, fold_sent, fold_got, gram_sent, gram_got,
-    load_sem, send_sem, own_sem, back_sem, get_sem, mate_send, mate_sem, gram_send, gram_sem, ready_sem,
+    load_sem, send_sem, own_sem, back_sem, get_sem, mate_send, mate_sem, pass_send, pass_sem, gram_send, gram_sem, ready_sem,
 ):
     island, row, col = (lax.axis_index(name) for name in ("island", "row", "col"))
     side, core = col // 2, col % 2
@@ -451,7 +451,19 @@
             sums_out[k, 0] = summed[0, k] + summed[0, partner[0, k]]
         for k in range(ISLANDS):
             sums_out[k, 1] = sums_out[partner[1, k], 0]
-        give_over_rows(2, sums_out, sums_in)
+
+        def give(index, carry):
+            k = far_island(index)
+            for near in range(2):
+                m = (row + 3 + side + near) % SIDE
+                pltpu.make_async_remote_copy(
+                    sums_out.at[k], sums_in.at[row, island // 2], back_sem.at[2], get_sem.at[2],
+                    device_id=device(k, m, other), device_id_type=MESH,
+                ).start()
+            return carry
+
+        lax.fori_loop(0, ISLANDS, give, 0, unroll=True)
+
 
     left_ref[:RANK, :] = 0.5 * exact_dot(near_inverse, near, PLAIN)
 
@@ -461,21 +473,48 @@
         for k in range(ISLANDS):
             last_out[k, 0] = summed[1, k] + summed[1, partner[1, k]]
         give_over_rows(3, last_out, last_in)
+
+    sized(arrived.at[0, pl.ds(0, TILES)], back_sem.at[2], get_sem.at[2]).wait_recv()
+    passed = []
+    for index, (source, target) in enumerate(
+        (((row + side) % SIDE, (row + 3) % SIDE), ((row + side + 3) % SIDE, (row + 1) % SIDE))
+    ):
+        copy = pltpu.make_async_remote_copy(
+            sums_in.at[source], sums_in.at[source], pass_send.at[index], pass_sem.at[index],
+            device_id=device(island, target, col), device_id_type=MESH,
+        )
+        copy.start()
+        passed.append(copy)
+
+    def whole_sums(which):
+        def tile(index):
+            k = index // 2
+            return sums_in[index % 2 * 2 + (k + core) % 2, k // 2, which]
+
+        return stack(
+            *(
+                jnp.concatenate([tile(a * BLOCKS + b) for b in range(BLOCKS)], axis=1)
+                for a in range(4)
+            )
+        )
 
     crossed = gram_finish()
     left_ref[RANK:, :] = 0.5 * exact_dot(eliminate(crossed, False)[:, :32], factor, PLAIN)
     near_change = -0.5 * exact_dot(crossed[:, 32:64], near_inverse, PLAIN)
     far_change = 0.5 * exact_dot(crossed[:, 64:96], far_inverse, PLAIN)
-    sized(sums_in, back_sem.at[2], get_sem.at[2]).wait_recv()
-    near_sums = whole(sums_in, 0)
+    for copy in passed:
+        copy.wait_recv()
+    near_sums = whole_sums(0)
     right_ref[:RANK, :] = near_sums
-    change = exact_dot(
-        jnp.concatenate([near_change, far_change], axis=1), stack(near_sums, whole(sums_in, 1)), PLAIN
+    change_high, change_low = halves(jnp.concatenate([near_change, far_change], axis=1))
+    sums_high, sums_low = halves(stack(near_sums, whole_sums(1)))
+    change = fast_dot(change_high, sums_high, PLAIN) + (
+        fast_dot(change_high, sums_low, PLAIN) + fast_dot(change_low, sums_high, PLAIN)
     )
     sized(last_in, back_sem.at[3], get_sem.at[3]).wait_recv()
     right_ref[RANK:, :] = whole(last_in, 0) + change
 
-    for copy in mate_copies:
+    for copy in mate_copies + passed:
         copy.wait_send()
     sized(arrived_first.at[pl.ds(0, 2 * SIDE - 1)], gram_send.at[0], gram_sem.at[0]).wait_send()
     sized(gram_got.at[pl.ds(0, SIDE - 1)], gram_send.at[1], gram_sem.at[1]).wait_send()
@@ -501,8 +540,8 @@
 
     @pl.when(col_owner)
     def _():
-        for flow, count in ((2, 2), (3, 1)):
-            sized(arrived.at[pl.ds(0, count)], back_sem.at[flow], get_sem.at[flow]).wait_send()
+        for flow in (2, 3):
+            sized(arrived.at[0], back_sem.at[flow], get_sem.at[flow]).wait_send()
 
 
 def update_kernel(weights_ref, left_ref, right_ref, out_ref, updated, sem):
@@ -544,13 +583,13 @@
             tiles(TILES, 2), tiles(PEERS, 2),
             tiles(2, TILES), tiles(2, PEERS), tiles(2, ISLANDS),
             tiles(2, ISLANDS, 2), tiles(ISLANDS, 1), tiles(ISLANDS, 2), tiles(ISLANDS, 1),
-            tiles(TILES, 2), tiles(TILES, 1), tiles(TILES, 2), tiles(TILES, 1),
+            tiles(TILES, 2), tiles(TILES, 1), tiles(SIDE, TILES // SIDE, 2), tiles(TILES, 1),
             pltpu.VMEM((2, RANK, WIDTH), jnp.float32),
             pltpu.VMEM((RANK // 2, 128), jnp.float32),
             pltpu.VMEM((2, SIDE, RANK // 2, 128), jnp.float32),
             pltpu.VMEM((RANK, 128), jnp.float32),
             pltpu.VMEM((SIDE, RANK, 128), jnp.float32),
-            dma((5,)), dma((3,)), dma((3,)), dma((4,)), dma((4,)), dma((2,)), dma((2,)), dma((2,)), dma((2,)),
+            dma((5,)), dma((3,)), dma((3,)), dma((4,)), dma((4,)), dma((2,)), dma((2,)), dma((2,)), dma((2,)), dma((2,)), dma((2,)),
             pltpu.SemaphoreType.REGULAR,
         ],
         compiler_params=pltpu.CompilerParams(

time: 51 us -> 50.2 us (0.984)
  Pallas kernels: 50.9 us -> 50.1 us
    pallas_call x1, Pallas kernels: 48.5 us -> 47.8 us  [shards(): pl.pallas_call(exchange_kernel, out_shape=(factors, factors, tile), in_sp...]
where the time goes in v6:
time: 50.2 us; the launch traced here: 50.1 us
  Pallas kernels  50.1 us (100%)
    pallas_call x1, Pallas kernels, shards(): pl.pallas_call(exchange_kernel, out_shape=(factors, factors, tile), in_sp...  47.8 us
    pallas_call x1, Pallas kernels, shards(): pl.pallas_call(update_kernel, out_shape=jax.ShapeDtypeStruct(weights.shap...  2.35 us

profile of v6, /device:TPU:1, one launch (start us, length us, event | category | flops | bytes accessed | tf_op | source)
XLA Modules:
  0.0 50.1 jit_solution(11360737723802355496)
XLA Ops:
  0.0 47.8 %exchange.1 = (f32[64,1024]{1,0:T(8,128)S(1)}, f32[64,1024]{1,0:T(8,128)S(1)}, f32[1024,1024]{1,0:T(8,128)S(1)}) custom-call(f32[1,1024,1024]{2,1,0:T(8,128)} %weights_ref.1, f32[2,32,1024]{2,1,0:T(8,128)} %bases_ref.1, s32[2,2,8]{2,1,0:T(2,128)} %bitcast.1), custom_call_target="tpu_custom_call" | custom-call | tf_op jit(solution)/shard_map/exchange/pallas_call | solution.py:573
  47.8 2.4 %update.1 = f32[1,1024,1024]{2,1,0:T(8,128)} custom-call(f32[1024,1024]{1,0:T(8,128)S(1)} %get-tuple-element.8.weights_ref, f32[64,1024]{1,0:T(8,128)S(1)} %get-tuple-element.9.left_ref, f32[64,1024]{1,0:T(8,128)S(1)} %get-tuple-element.10.right_ref), custom_call_target="tpu_custom_call" | custom-call | tf_op jit(solution)/shard_map/update/pallas_call | solution.py:601

commit v7 on v6

--- a/solution.py
+++ b/solution.py
@@ -13,7 +13,7 @@
 ISLANDS = 16
 SIDE = 4
 PEERS = ISLANDS * SIDE
-BLOCK = 4
+BLOCK = 8
 HIGHEST = lax.Precision.HIGHEST
 LAST = (((1,), (1,)), ((), ()))
 FIRST = (((0,), (0,)), ((), ()))
@@ -88,7 +88,7 @@
     high_ref, low_ref, bases_in, partner, first, arrived_first, sent, arrived, summed,
     pair_out, late_out, sums_out, last_out, pair_in, late_in, sums_in, last_in,
     factors_in, fold_sent, fold_got, gram_sent, gram_got,
-    load_sem, send_sem, own_sem, back_sem, get_sem, mate_send, mate_sem, pass_send, pass_sem, gram_send, gram_sem, ready_sem,
+    load_sem, send_sem, own_sem, back_sem, get_sem, mate_send, mate_sem, pass_send, pass_sem, gram_send, gram_sem,
 ):
     island, row, col = (lax.axis_index(name) for name in ("island", "row", "col"))
     side, core = col // 2, col % 2
@@ -115,17 +115,22 @@
     def far_island(index):
         return (across + far_first(index // SIDE)) % SIDE * SIDE + (along + far_first(index % SIDE)) % SIDE
 
-    def greet(index, carry):
-        k = far_island(index)
-        for m in range(SIDE):
-
-            @pl.when((k != island) | (m != col))
-            def _():
-                pl.semaphore_signal(barrier, inc=1, device_id=device(k, row, m), device_id_type=MESH)
-
-        return carry
-
-    lax.fori_loop(0, ISLANDS, greet, 0, unroll=True)
+    row_owner = core == island % 2
+
+    @pl.when(row_owner)
+    def _():
+        def greet(index, carry):
+            k = far_island(index)
+            for m in range(SIDE):
+
+                @pl.when((k != island) | (m != col))
+                def _():
+                    pl.semaphore_signal(barrier, inc=1, device_id=device(k, row, m), device_id_type=MESH)
+
+            return carry
+
+        lax.fori_loop(0, ISLANDS, greet, 0, unroll=True)
+
     for step in range(1, SIDE):
         pl.semaphore_signal(
             barrier, inc=1, device_id=device(island, (row + step) % SIDE, col), device_id_type=MESH
@@ -159,13 +164,8 @@
         terms = wide[: 2 * RANK] + (wide[2 * RANK :] + fine)
         put_first(terms, part)
 
-    pl.semaphore_wait(barrier, PEERS - 1 + SIDE - 1)
-    for step in range(1, SIDE):
-        pl.semaphore_signal(
-            ready_sem, inc=1, device_id=device(island, (row + step) % SIDE, col), device_id_type=MESH
-        )
-
-    row_owner = core == island % 2
+    pl.semaphore_wait(barrier, TILES - row_owner.astype(jnp.int32) + SIDE - 1)
+
     row_tile = island * 2 + side
     col_owner = row % 2 == (island + core) % 2
     col_tile = island * 2 + row // 2
@@ -393,7 +393,6 @@
         near_product.append(value)
 
     times_weights(near_high, near_low, RANK, use_near)
-    pl.semaphore_wait(ready_sem, SIDE - 1)
     send_over_rows(0)
     mate_copies[1].wait_recv()
     late = whole(late_in, 0)
@@ -590,7 +589,6 @@
             pltpu.VMEM((RANK, 128), jnp.float32),
             pltpu.VMEM((SIDE, RANK, 128), jnp.float32),
             dma((5,)), dma((3,)), dma((3,)), dma((4,)), dma((4,)), dma((2,)), dma((2,)), dma((2,)), dma((2,)), dma((2,)), dma((2,)),
-            pltpu.SemaphoreType.REGULAR,
         ],
         compiler_params=pltpu.CompilerParams(
             collective_id=0, has_side_effects=True, vmem_limit_bytes=32 * 2**20

time: 50.2 us -> 49.2 us (0.980)
  Pallas kernels: 50.1 us -> 48.9 us
    pallas_call x1, Pallas kernels: 47.8 us -> 46.6 us  [shards(): pl.pallas_call(exchange_kernel, out_shape=(factors, factors, tile), in_sp...]
where the time goes in v7:
time: 49.2 us; the launch traced here: 48.9 us
  Pallas kernels  48.9 us (99%)
    pallas_call x1, Pallas kernels, shards(): pl.pallas_call(exchange_kernel, out_shape=(factors, factors, tile), in_sp...  46.6 us
    pallas_call x1, Pallas kernels, shards(): pl.pallas_call(update_kernel, out_shape=jax.ShapeDtypeStruct(weights.shap...  2.33 us

profile of v7, /device:TPU:1, one launch (start us, length us, event | category | flops | bytes accessed | tf_op | source)
XLA Modules:
  0.0 48.9 jit_solution(4469137556542422638)
XLA Ops:
  0.0 46.6 %exchange.1 = (f32[64,1024]{1,0:T(8,128)S(1)}, f32[64,1024]{1,0:T(8,128)S(1)}, f32[1024,1024]{1,0:T(8,128)S(1)}) custom-call(f32[1,1024,1024]{2,1,0:T(8,128)} %weights_ref.1, f32[2,32,1024]{2,1,0:T(8,128)} %bases_ref.1, s32[2,2,8]{2,1,0:T(2,128)} %bitcast.1), custom_call_target="tpu_custom_call" | custom-call | tf_op jit(solution)/shard_map/exchange/pallas_call | solution.py:572
  46.6 2.3 %update.1 = f32[1,1024,1024]{2,1,0:T(8,128)} custom-call(f32[1024,1024]{1,0:T(8,128)S(1)} %get-tuple-element.8.weights_ref, f32[64,1024]{1,0:T(8,128)S(1)} %get-tuple-element.9.left_ref, f32[64,1024]{1,0:T(8,128)S(1)} %get-tuple-element.10.right_ref), custom_call_target="tpu_custom_call" | custom-call | tf_op jit(solution)/shard_map/update/pallas_call | solution.py:599

commit v8 on v7

--- a/solution.py
+++ b/solution.py
@@ -115,26 +115,26 @@
     def far_island(index):
         return (across + far_first(index // SIDE)) % SIDE * SIDE + (along + far_first(index % SIDE)) % SIDE
 
-    row_owner = core == island % 2
-
-    @pl.when(row_owner)
-    def _():
-        def greet(index, carry):
-            k = far_island(index)
-            for m in range(SIDE):
-
-                @pl.when((k != island) | (m != col))
-                def _():
-                    pl.semaphore_signal(barrier, inc=1, device_id=device(k, row, m), device_id_type=MESH)
-
-            return carry
-
-        lax.fori_loop(0, ISLANDS, greet, 0, unroll=True)
-
     for step in range(1, SIDE):
         pl.semaphore_signal(
             barrier, inc=1, device_id=device(island, (row + step) % SIDE, col), device_id_type=MESH
         )
+
+    row_owner = core == island % 2
+
+    @pl.when(row_owner)
+    def _():
+        def greet(index, carry):
+            k = far_island(index)
+            for m in range(SIDE):
+
+                @pl.when((k != island) | (m != col))
+                def _():
+                    pl.semaphore_signal(barrier, inc=1, device_id=device(k, row, m), device_id_type=MESH)
+
+            return carry
+
+        lax.fori_loop(0, ISLANDS, greet, 0, unroll=True)
 
     base_load.wait()
     base_high, base_low = halves(bases_in[...].reshape(2 * RANK, WIDTH))
@@ -256,16 +256,16 @@
 
     def give_over_rows(flow, out, into):
         def give(index, carry):
-            k = far_island(index % ISLANDS)
-            for near in range(2):
-                m = (row + 1 + side + near + 2 * (index // ISLANDS)) % SIDE
+            k = far_island(index)
+            for near in range(SIDE):
+                m = (row + 1 + side + near) % SIDE
                 pltpu.make_async_remote_copy(
                     out.at[k], into.at[col_tile], back_sem.at[flow], get_sem.at[flow],
                     device_id=device(k, m, other), device_id_type=MESH,
                 ).start()
             return carry
 
-        lax.fori_loop(0, 2 * ISLANDS, give, 0, unroll=True)
+        lax.fori_loop(0, ISLANDS, give, 0, unroll=True)
 
     def whole(ref, which):
         return stack(
@@ -419,16 +419,36 @@
     near_inverse, far_inverse = solved[:, :32], solved[:, 64:96]
     mixing = 0.5 * stack(-solved[:, 32:64], solved[:, 96:128])
     mixing_high, mixing_low = halves(mixing)
+    mixing_stack = stack(mixing_high, mixing_high, mixing_low)
 
     def mixed(high, low):
-        return fast_dot(mixing_high, high, FIRST) + (
-            fast_dot(mixing_high, low, FIRST) + fast_dot(mixing_low, high, FIRST)
-        )
+        return fast_dot(mixing_stack, stack(high, low, high), FIRST)
 
     terms = later[:RANK] + mixed(product_high, product_low)
     for part in range(4):
         put(1, terms[:, part * 256 : part * 256 + 256], part)
     send_over_rows(1)
+
+    @pl.when(col_owner)
+    def _():
+        owned_over_rows(0)
+        for k in range(ISLANDS):
+            sums_out[k, 0] = summed[0, k] + summed[0, partner[0, k]]
+        for k in range(ISLANDS):
+            sums_out[k, 1] = sums_out[partner[1, k], 0]
+
+        def give(index, carry):
+            k = far_island(index)
+            for near in range(2):
+                m = (row + 3 + side + near) % SIDE
+                pltpu.make_async_remote_copy(
+                    sums_out.at[k], sums_in.at[row, island // 2], back_sem.at[2], get_sem.at[2],
+                    device_id=device(k, m, other), device_id_type=MESH,
+                ).start()
+            return carry
+
+        lax.fori_loop(0, ISLANDS, give, 0, unroll=True)
+
 
     factor = late + mixed(stack(near_high, far_high), stack(near_low, far_low))
     factor_high, factor_low = halves(factor)
@@ -442,27 +462,6 @@
         LAST,
     )
     gram_start(block[:RANK, :128] + (block[:RANK, 128:] + block[RANK:, :128]))
-
-    @pl.when(col_owner)
-    def _():
-        owned_over_rows(0)
-        for k in range(ISLANDS):
-            sums_out[k, 0] = summed[0, k] + summed[0, partner[0, k]]
-        for k in range(ISLANDS):
-            sums_out[k, 1] = sums_out[partner[1, k], 0]
-
-        def give(index, carry):
-            k = far_island(index)
-            for near in range(2):
-                m = (row + 3 + side + near) % SIDE
-                pltpu.make_async_remote_copy(
-                    sums_out.at[k], sums_in.at[row, island // 2], back_sem.at[2], get_sem.at[2],
-                    device_id=device(k, m, other), device_id_type=MESH,
-                ).start()
-            return carry
-
-        lax.fori_loop(0, ISLANDS, give, 0, unroll=True)
-
 
     left_ref[:RANK, :] = 0.5 * exact_dot(near_inverse, near, PLAIN)
 

time: 49.2 us -> 49.2 us (level)
  no operation moved by 1% of the time
where the time goes in v8:
time: 49.2 us; the launch traced here: 48.5 us
  Pallas kernels  48.5 us (99%)
    pallas_call x1, Pallas kernels, shards(): pl.pallas_call(exchange_kernel, out_shape=(factors, factors, tile), in_sp...  46.1 us
    pallas_call x1, Pallas kernels, shards(): pl.pallas_call(update_kernel, out_shape=jax.ShapeDtypeStruct(weights.shap...  2.34 us

profile of v8, /device:TPU:1, one launch (start us, length us, event | category | flops | bytes accessed | tf_op | source)
XLA Modules:
  0.0 48.5 jit_solution(2647061498971515163)
XLA Ops:
  0.0 46.1 %exchange.1 = (f32[64,1024]{1,0:T(8,128)S(1)}, f32[64,1024]{1,0:T(8,128)S(1)}, f32[1024,1024]{1,0:T(8,128)S(1)}) custom-call(f32[1,1024,1024]{2,1,0:T(8,128)} %weights_ref.1, f32[2,32,1024]{2,1,0:T(8,128)} %bases_ref.1, s32[2,2,8]{2,1,0:T(2,128)} %bitcast.1), custom_call_target="tpu_custom_call" | custom-call | tf_op jit(solution)/shard_map/exchange/pallas_call | solution.py:571
  46.2 2.3 %update.1 = f32[1,1024,1024]{2,1,0:T(8,128)} custom-call(f32[1024,1024]{1,0:T(8,128)S(1)} %get-tuple-element.8.weights_ref, f32[64,1024]{1,0:T(8,128)S(1)} %get-tuple-element.9.left_ref, f32[64,1024]{1,0:T(8,128)S(1)} %get-tuple-element.10.right_ref), custom_call_target="tpu_custom_call" | custom-call | tf_op jit(solution)/shard_map/update/pallas_call | solution.py:598
